TPU v7x, 32 devices: a whole 2x2x4 slice. The times are simulated.
32 devices in a mesh: dp: 8 (over z, x), fsdp: 4 (over y, core).
Axes of the slice: x: 2, y: 2, z: 4, core: 2. Of those that a mesh axis runs over, the one named last changes fastest.
Arguments:
- query_tokens: bfloat16 [128, 128, 768], P(('dp', 'fsdp')), may hold values from -6 to 6
- passage_tokens: bfloat16 [32, 512, 768], P(('dp', 'fsdp')), may hold values from -6 to 6
- query_lengths: int32 [128], P(('dp', 'fsdp')), may hold values from 0 to 128, as said below
- passage_lengths: int32 [32], P(('dp', 'fsdp')), may hold values from 0 to 512, as said below
- query_cotangent: bfloat16 [128, 128, 768], P(('dp', 'fsdp')), may hold values from -6 to 6
- passage_cotangent: bfloat16 [32, 512, 768], P(('dp', 'fsdp')), may hold values from -6 to 6
- qkv_weight: bfloat16 [768, 2304], P(('dp', 'fsdp')), may hold values from -0.21875 to 0.21875
- out_weight: bfloat16 [768, 768], P(('dp', 'fsdp')), may hold values from -1.75 to 1.75
- inner_weight: bfloat16 [768, 3072], P(('dp', 'fsdp')), may hold values from -0.21875 to 0.21875
- outer_weight: bfloat16 [3072, 768], P(('dp', 'fsdp')), may hold values from -0.109375 to 0.109375
- ln_gains: bfloat16 [2, 768], P(None, ('dp', 'fsdp')), may hold values from 0.5 to 1.5
- bias_rows: bfloat16 [6, 768], P(None, ('dp', 'fsdp')), may hold values from -3 to 3
- inner_bias: bfloat16 [3072], P(('dp', 'fsdp')), may hold values from -3 to 3
Outputs:
- query_out: bfloat16 [128, 128, 768], P(('dp', 'fsdp'))
- passage_out: bfloat16 [32, 512, 768], P(('dp', 'fsdp'))
- query_grad: bfloat16 [128, 128, 768], P(('dp', 'fsdp'))
- passage_grad: bfloat16 [32, 512, 768], P(('dp', 'fsdp'))
- grad_qkv: float32 [768, 2304], P(('dp', 'fsdp'))
- grad_out: float32 [768, 768], P(('dp', 'fsdp'))
- grad_inner: float32 [768, 3072], P(('dp', 'fsdp'))
- grad_outer: float32 [3072, 768], P(('dp', 'fsdp'))
- grad_gains: float32 [2, 768], P(None, ('dp', 'fsdp'))
- grad_biases: float32 [6, 768], P(None, ('dp', 'fsdp'))
- grad_inner_bias: float32 [3072], P(('dp', 'fsdp'))
Inputs may be any that keep to these rules, and one draw needn't show every extreme that they name: `query_lengths`: on each device the used slots of its 4 query slots come first; every device uses at least 2, some device all of them. A used slot holds 64 to 128 real tokens, an unused one 0; some sequence has exactly 128. `passage_lengths`: on each device the used slots of its 1 passage slots come first; every device uses at least 0, some device all of them. A used slot holds 256 to 512 real tokens, an unused one 0; some sequence has exactly 512.
All inputs are finite; a program needn't handle non-finite values.
Results may differ from a plain program's by a relative error of at most 0.014.
Values may be sent and summed in bfloat16 or wider, within the bound.
No kernel may reach another device: no remote copies, remote signals or barrier semaphores. Data moves between devices by JAX's collectives and lax.ppermute only.
A program may use at most 192 MiB of HBM per device.

v0:
```python
import jax
import jax.numpy as jnp
from jax import lax
from jax.sharding import PartitionSpec as P

HEADS = 12


EPSILON = 1e-12
MASKED = -1000000000.0


def layer_norm(hidden, gain_vec, shift_vec):
    center = hidden - jnp.mean(hidden, axis=-1, keepdims=True)
    spread = jnp.mean(center * center, axis=-1, keepdims=True)
    return center * lax.rsqrt(spread + EPSILON) * gain_vec + shift_vec


def exact_gelu(value):
    return jax.nn.gelu(value, approximate=False)


def row_valid(lengths, seq_length):
    return jnp.arange(seq_length)[None, :] < lengths[:, None]


def split_heads(qkv_rows):
    seq_count, seq_length, triple = qkv_rows.shape
    heads_view = qkv_rows.reshape(seq_count, seq_length, 3, HEADS, triple // (3 * HEADS))
    return (heads_view[:, :, 0], heads_view[:, :, 1], heads_view[:, :, 2])


def attn_scores(queries, keys_all, valid_rows):
    scores = (
        jnp.einsum("blhe,bmhe->bhlm", queries, keys_all, preferred_element_type=jnp.float32) * 0.125
    )
    return jnp.where(valid_rows[:, None, None, :], scores, MASKED)


def attend(qkv_rows, lengths):
    queries, keys_all, values = split_heads(qkv_rows)
    valid_rows = row_valid(lengths, qkv_rows.shape[1])
    scores = attn_scores(queries, keys_all, valid_rows)
    highest = jnp.max(scores, axis=-1, keepdims=True)
    exponent = jnp.exp(scores - highest)
    total = jnp.sum(exponent, axis=-1, keepdims=True)
    weights = (exponent / total).astype(jnp.bfloat16)
    context = jnp.einsum("bhlm,bmhe->blhe", weights, values, preferred_element_type=jnp.float32)
    flat_context = context.reshape(qkv_rows.shape[0], qkv_rows.shape[1], -1).astype(jnp.bfloat16)
    return (flat_context, highest + jnp.log(total))


def attend_back(qkv_rows, lengths, log_total, grad_context):
    queries, keys_all, values = split_heads(qkv_rows)
    valid_rows = row_valid(lengths, qkv_rows.shape[1])
    scores = attn_scores(queries, keys_all, valid_rows)
    probs = jnp.exp(scores - log_total)
    probs_low = probs.astype(jnp.bfloat16)
    grad_heads = grad_context.reshape(queries.shape)
    grad_values = jnp.einsum(
        "bhlm,blhe->bmhe", probs_low, grad_heads, preferred_element_type=jnp.float32
    )
    grad_probs = jnp.einsum(
        "blhe,bmhe->bhlm", grad_heads, values, preferred_element_type=jnp.float32
    )
    grad_scores = probs * (grad_probs - jnp.sum(grad_probs * probs, axis=-1, keepdims=True))
    grad_scores = jnp.where(valid_rows[:, None, None, :], grad_scores, 0.0).astype(jnp.bfloat16)
    grad_queries = (
        jnp.einsum("bhlm,bmhe->blhe", grad_scores, keys_all, preferred_element_type=jnp.float32)
        * 0.125
    )
    grad_keys = (
        jnp.einsum("bhlm,blhe->bmhe", grad_scores, queries, preferred_element_type=jnp.float32)
        * 0.125
    )
    flat_shape = qkv_rows.shape[:2] + (-1,)
    return jnp.concatenate(
        [
            grad_queries.reshape(flat_shape),
            grad_keys.reshape(flat_shape),
            grad_values.reshape(flat_shape),
        ],
        axis=-1,
    )


def per_device(
    query_tokens,
    passage_tokens,
    query_lengths,
    passage_lengths,
    query_cotangent,
    passage_cotangent,
    qkv_weight,
    out_weight,
    inner_weight,
    outer_weight,
    ln_gains,
    bias_rows,
    inner_bias,
):
    owned = (qkv_weight, out_weight, inner_weight, outer_weight, ln_gains, bias_rows, inner_bias)
    gathered = (
        lax.all_gather(owned[0], ("dp", "fsdp"), axis=0, tiled=True),
        lax.all_gather(owned[1], ("dp", "fsdp"), axis=0, tiled=True),
        lax.all_gather(owned[2], ("dp", "fsdp"), axis=0, tiled=True),
        lax.all_gather(owned[3], ("dp", "fsdp"), axis=0, tiled=True),
        lax.all_gather(owned[4], ("dp", "fsdp"), axis=1, tiled=True),
        lax.all_gather(owned[5], ("dp", "fsdp"), axis=1, tiled=True),
        lax.all_gather(owned[6], ("dp", "fsdp"), axis=0, tiled=True),
    )
    full_qkv, full_out, full_inner, full_outer, full_gains, full_biases, full_inner_bias = gathered
    gain_rows = full_gains.astype(jnp.float32)
    bias_vals = full_biases.astype(jnp.float32)
    inner_shift = full_inner_bias.astype(jnp.float32)
    query_count, query_length, model_width = query_tokens.shape
    passage_count, passage_length = passage_tokens.shape[:2]
    query_rows = query_count * query_length
    token_rows = jnp.concatenate(
        [query_tokens.reshape(query_rows, model_width), passage_tokens.reshape(-1, model_width)],
        axis=0,
    )
    qkv_shift = jnp.concatenate(
        [bias_vals[0], jnp.zeros((model_width,), jnp.float32), bias_vals[1]]
    )
    qkv_rows = (
        jnp.dot(token_rows, full_qkv, preferred_element_type=jnp.float32) + qkv_shift
    ).astype(jnp.bfloat16)
    query_qkv = qkv_rows[:query_rows].reshape(query_count, query_length, -1)
    passage_qkv = qkv_rows[query_rows:].reshape(passage_count, passage_length, -1)
    query_context, query_lse = attend(query_qkv, query_lengths)
    passage_context, passage_lse = attend(passage_qkv, passage_lengths)
    context = jnp.concatenate(
        [query_context.reshape(-1, model_width), passage_context.reshape(-1, model_width)], axis=0
    )
    attended = jnp.dot(context, full_out, preferred_element_type=jnp.float32) + bias_vals[2]
    normed, norm_first_back = jax.vjp(
        layer_norm, token_rows.astype(jnp.float32) + attended, gain_rows[0], bias_vals[3]
    )
    normed_low = normed.astype(jnp.bfloat16)
    upward = jnp.dot(normed_low, full_inner, preferred_element_type=jnp.float32) + inner_shift
    activated, gelu_back = jax.vjp(exact_gelu, upward)
    activated_low = activated.astype(jnp.bfloat16)
    downward = jnp.dot(activated_low, full_outer, preferred_element_type=jnp.float32) + bias_vals[4]
    result, norm_second_back = jax.vjp(layer_norm, normed + downward, gain_rows[1], bias_vals[5])
    valid_tokens = jnp.concatenate(
        [
            row_valid(query_lengths, query_length).reshape(-1),
            row_valid(passage_lengths, passage_length).reshape(-1),
        ],
        axis=0,
    )[:, None]
    output_rows = jnp.where(valid_tokens, result, 0.0).astype(jnp.bfloat16)
    back_qkv, back_out, back_inner, back_outer = (
        lax.all_gather(qkv_weight, ("dp", "fsdp"), axis=0, tiled=True),
        lax.all_gather(out_weight, ("dp", "fsdp"), axis=0, tiled=True),
        lax.all_gather(inner_weight, ("dp", "fsdp"), axis=0, tiled=True),
        lax.all_gather(outer_weight, ("dp", "fsdp"), axis=0, tiled=True),
    )
    cot_rows = jnp.concatenate(
        [query_cotangent.reshape(-1, model_width), passage_cotangent.reshape(-1, model_width)],
        axis=0,
    ).astype(jnp.float32)
    grad_result = jnp.where(valid_tokens, cot_rows, 0.0)
    grad_second, grad_gain_two, grad_shift_two = norm_second_back(grad_result)
    grad_down_low = grad_second.astype(jnp.bfloat16)
    weight_outer = jnp.einsum(
        "rf,rd->fd", activated_low, grad_down_low, preferred_element_type=jnp.float32
    )
    grad_activated = jnp.einsum(
        "rd,fd->rf", grad_down_low, back_outer, preferred_element_type=jnp.float32
    )
    (grad_upward,) = gelu_back(grad_activated)
    grad_up_low = grad_upward.astype(jnp.bfloat16)
    weight_inner = jnp.einsum(
        "rd,rf->df", normed_low, grad_up_low, preferred_element_type=jnp.float32
    )
    grad_normed = grad_second + jnp.einsum(
        "rf,df->rd", grad_up_low, back_inner, preferred_element_type=jnp.float32
    )
    grad_first, grad_gain_one, grad_shift_one = norm_first_back(grad_normed)
    grad_attn_low = grad_first.astype(jnp.bfloat16)
    weight_out = jnp.einsum("rc,rd->cd", context, grad_attn_low, preferred_element_type=jnp.float32)
    grad_context = jnp.einsum(
        "rd,cd->rc", grad_attn_low, back_out, preferred_element_type=jnp.float32
    ).astype(jnp.bfloat16)
    query_grad_qkv = attend_back(
        query_qkv,
        query_lengths,
        query_lse,
        grad_context[:query_rows].reshape(query_count, query_length, -1),
    )
    passage_grad_qkv = attend_back(
        passage_qkv,
        passage_lengths,
        passage_lse,
        grad_context[query_rows:].reshape(passage_count, passage_length, -1),
    )
    grad_qkv = jnp.concatenate(
        [query_grad_qkv.reshape(query_rows, -1), passage_grad_qkv.reshape(-1, 3 * model_width)],
        axis=0,
    )
    grad_qkv_low = grad_qkv.astype(jnp.bfloat16)
    weight_qkv = jnp.einsum(
        "rd,re->de", token_rows, grad_qkv_low, preferred_element_type=jnp.float32
    )
    grad_inputs = (
        grad_first
        + jnp.einsum("re,de->rd", grad_qkv_low, back_qkv, preferred_element_type=jnp.float32)
    ).astype(jnp.bfloat16)
    gain_terms = jnp.stack([grad_gain_one, grad_gain_two])
    bias_terms = jnp.stack(
        [
            jnp.sum(grad_qkv[:, :model_width], axis=0),
            jnp.sum(grad_qkv[:, 2 * model_width :], axis=0),
            jnp.sum(grad_first, axis=0),
            grad_shift_one,
            jnp.sum(grad_second, axis=0),
            grad_shift_two,
        ]
    )
    inner_terms = jnp.sum(grad_upward, axis=0)
    terms = (
        weight_qkv,
        weight_out,
        weight_inner,
        weight_outer,
        gain_terms,
        bias_terms,
        inner_terms,
    )
    owned_grads = (
        lax.psum_scatter(terms[0], ("dp", "fsdp"), scatter_dimension=0, tiled=True),
        lax.psum_scatter(terms[1], ("dp", "fsdp"), scatter_dimension=0, tiled=True),
        lax.psum_scatter(terms[2], ("dp", "fsdp"), scatter_dimension=0, tiled=True),
        lax.psum_scatter(terms[3], ("dp", "fsdp"), scatter_dimension=0, tiled=True),
        lax.psum_scatter(terms[4], ("dp", "fsdp"), scatter_dimension=1, tiled=True),
        lax.psum_scatter(terms[5], ("dp", "fsdp"), scatter_dimension=1, tiled=True),
        lax.psum_scatter(terms[6], ("dp", "fsdp"), scatter_dimension=0, tiled=True),
    )
    query_out = output_rows[:query_rows].reshape(query_tokens.shape)
    passage_out = output_rows[query_rows:].reshape(passage_tokens.shape)
    query_grad = grad_inputs[:query_rows].reshape(query_tokens.shape)
    passage_grad = grad_inputs[query_rows:].reshape(passage_tokens.shape)
    return (
        query_out,
        passage_out,
        query_grad,
        passage_grad,
        owned_grads[0],
        owned_grads[1],
        owned_grads[2],
        owned_grads[3],
        owned_grads[4],
        owned_grads[5],
        owned_grads[6],
    )


def solution(mesh):
    in_specs = (
        P(("dp", "fsdp"), None, None),
        P(("dp", "fsdp"), None, None),
        P(("dp", "fsdp")),
        P(("dp", "fsdp")),
        P(("dp", "fsdp"), None, None),
        P(("dp", "fsdp"), None, None),
        P(("dp", "fsdp"), None),
        P(("dp", "fsdp"), None),
        P(("dp", "fsdp"), None),
        P(("dp", "fsdp"), None),
        P(None, ("dp", "fsdp")),
        P(None, ("dp", "fsdp")),
        P(("dp", "fsdp")),
    )
    out_specs = (
        P(("dp", "fsdp"), None, None),
        P(("dp", "fsdp"), None, None),
        P(("dp", "fsdp"), None, None),
        P(("dp", "fsdp"), None, None),
        P(("dp", "fsdp"), None),
        P(("dp", "fsdp"), None),
        P(("dp", "fsdp"), None),
        P(("dp", "fsdp"), None),
        P(None, ("dp", "fsdp")),
        P(None, ("dp", "fsdp")),
        P(("dp", "fsdp")),
    )
    return jax.shard_map(
        per_device, mesh=mesh, in_specs=in_specs, out_specs=out_specs, check_vma=False
    )
```

profile of v0, /device:TPU:16, one launch (start us, length us, event | category | flops | bytes accessed | tf_op | source)
XLA Modules:
  0.0 831.7 jit_solution(15654625334405486995)
XLA Ops:
  12.3 40.6 %all-reduce = bf16[3072]{0:T(1024)(128)(2,1)S(1)} all-reduce(bf16[3072]{0:T(1024)(128)(2,1)S(1)} %dynamic-update-slice), channel_id=1, replica_groups=mesh['dp'=8,'fsdp'=4] {'dp','fsdp'}, use_global_device_ids=true, to_apply=%add | all-reduce | flops 3072 | bytes 12288
  52.9 31.6 %all-gather.1 = bf16[32,24,2]{1,2,0:T(2,128)(2,1)S(1)} all-gather(bf16[1,24,2]{1,2,0:T(2,128)(2,1)} %bitcast.166), channel_id=1, replica_groups=mesh['dp'=8,'fsdp'=4] {'dp','fsdp'}, dimensions={0}, use_global_device_ids=true | all-gather | bytes 3168 | tf_op jit(solution)/shard_map/all_gather | solution.py:108
  85.4 33.0 %all-gather = bf16[32,24,6]{1,2,0:T(8,128)(2,1)S(1)} all-gather(bf16[1,24,6]{1,2,0:T(8,128)(2,1)} %bitcast.165), channel_id=1, replica_groups=mesh['dp'=8,'fsdp'=4] {'dp','fsdp'}, dimensions={0}, use_global_device_ids=true | all-gather | bytes 9504 | tf_op jit(solution)/shard_map/all_gather | solution.py:109
  119.9 6.3 add_convert_fusion
  130.4 4.2 reshape_reshape.12
  154.4 4.2 fusion.92
  158.6 4.0 fusion.136
  164.4 28.8 %all-gather.11.cloned.1.call-done = bf16[768,3072]{1,0:T(8,128)(2,1)} async-done(((bf16[24,3072]{1,0:T(8,128)(2,1)}), bf16[768,3072]{1,0:T(8,128)(2,1)}) %all-gather.11.cloned.1.call-update) | async-done | bytes 4718608 | tf_op jit(solution)/shard_map/all_gather | solution.py:106
  193.2 35.8 %multiply_convert_fusion = (bf16[1024,3072]{1,0:T(8,128)(2,1)}, f32[1024,3072]{1,0:T(8,128)}, f32[1024,3072]{1,0:T(8,128)}) fusion(f32[3072]{0:T(1024)S(1)} %convert_element_type.105, bf16[768,3072]{1,0:T(8,128)(2,1)} %all-gather.11.cloned.1.call-done, f32[1024,768]{1,0:T(8,128)S(1)} %get-tuple-element.55, f32[768]{0:T(1024)S(1)} %get-tuple-element.21, ...), kind=kOutput, calls=%fused_computation.9 | convolution fusion | flops 5043388416 | bytes 39348224 | tf_op jit(solution)/shard_map/dot_general | solution.py:141
  229.0 29.4 %all-gather.13.cloned.1.call-done = bf16[3072,768]{1,0:T(8,128)(2,1)} async-done(((bf16[96,768]{1,0:T(8,128)(2,1)}), bf16[3072,768]{1,0:T(8,128)(2,1)}) %all-gather.13.cloned.1.call-update) | async-done | bytes 4718608 | tf_op jit(solution)/shard_map/all_gather | solution.py:107
  258.4 8.8 %fusion.137 = (f32[1024]{0:T(1024)S(1)}, f32[1024,768]{1,0:T(8,128)S(1)}) fusion(f32[768]{0:T(1024)S(1)} %get-tuple-element.20, bf16[1024,3072]{1,0:T(8,128)(2,1)} %get-tuple-element.34, bf16[3072,768]{1,0:T(8,128)(2,1)} %all-gather.13.cloned.1.call-done, f32[768]{0:T(1024)S(1)} %get-tuple-element.21, f32[768]{0:T(1024)S(1)} %get-tuple-element.26, ...), kind=kOutput, calls=%fused_computation.182 | convolution fusion | flops 4837342208 | bytes 17323008 | tf_op jit(solution)/shard_map/dot_general | solution.py:144
  270.9 4.1 fusion.130
  275.1 19.2 %fusion.138 = (f32[3072]{0:T(1024)S(1)}, bf16[1024,3072]{1,0:T(8,128)(2,1)}) fusion(f32[1024,3072]{1,0:T(8,128)} %get-tuple-element.35, bf16[3072,768]{1,0:T(8,128)(2,1)} %all-gather.13.cloned.1.call-done, f32[1024,768]{1,0:T(8,128)} %get-tuple-element.33, f32[1024]{0:T(1024)S(1)} %negate_multiply_fusion.2, f32[1024,3072]{1,0:T(8,128)} %get-tuple-element.56, ...), kind=kOutput, calls=%fused_computation.183 | convolution fusion | flops 4883739648 | bytes 39350272 | tf_op jit(solution)/shard_map/rd,fd->rf/dot_general | solution.py:170
  294.3 10.0 %multiply_reduce_fusion.2 = (f32[768]{0:T(1024)S(1)}, f32[1024]{0:T(1024)S(1)}, f32[768]{0:T(1024)S(1)}, f32[1024,768]{1,0:T(8,128)S(1)}) fusion(f32[1024,768]{1,0:T(8,128)S(1)} %get-tuple-element.55, f32[1024]{0:T(1024)S(1)} %fusion.102, f32[1024]{0:T(1024)S(1)} %broadcast_multiply_fusion.1, f32[768]{0:T(1024)S(1)} %get-tuple-element.26, ...), kind=kOutput, calls=%fused_computation.52 | convolution fusion | flops 4839699456 | bytes 20472832 | tf_op jit(solution)/shard_map/rf,df->rd/dot_general | solution.py:178
  310.5 3.7 convolution_convert_fusion
  318.2 3.9 fusion.97
  324.5 7.6 multiply_bitcast_fusion.1
  332.1 7.7 fusion.98
  339.8 7.6 multiply_bitcast_fusion
  347.4 3.8 copy.101
  355.7 21.0 %fusion.85 = f32[12,64,512]{2,1,0:T(8,128)} fusion(f32[12,512,512]{1,2,0:T(8,128)} %fusion.98, f32[12,512,512]{1,2,0:T(8,128)} %copy-done, f32[12,512]{1,0:T(8,128)S(1)} %copy-done.26, pred[512]{0:T(512)(128)(4,1)S(1)} %copy-done.30, bf16[1,512,3,12,64]{1,4,3,2,0:T(8,128)(2,1)} %bitcast.141), kind=kOutput, calls=%fused_computation.109 | convolution fusion | flops 437656064 | bytes 52757504 | tf_op jit(solution)/shard_map/bhlm,bmhe->blhe/dot_general | solution.py:69
  376.7 20.9 %fusion.88 = f32[12,64,512]{2,1,0:T(8,128)} fusion(f32[12,512,512]{1,2,0:T(8,128)} %fusion.98, f32[12,512,512]{1,2,0:T(8,128)} %copy-done, f32[12,512]{1,0:T(8,128)S(1)} %copy-done.26, pred[512]{0:T(512)(128)(4,1)S(1)} %copy-done.30, bf16[1,512,3,12,64]{1,4,3,2,0:T(8,128)(2,1)} %bitcast.142), kind=kOutput, calls=%fused_computation.110 | convolution fusion | flops 437656064 | bytes 52757504 | tf_op jit(solution)/shard_map/bhlm,blhe->bmhe/dot_general | solution.py:73
  399.9 7.4 fusion.34
  410.1 8.3 %fusion.54 = f32[768,2304]{1,0:T(8,128)} fusion(bf16[512,768]{1,0:T(8,128)(2,1)S(1)} %bitcast.169, bf16[512,768]{1,0:T(8,128)(2,1)S(1)} %bitcast.172, f32[512,2304]{0,1:T(8,128)S(1)} %maximum_bitcast_fusion, f32[512,768]{0,1:T(8,128)S(1)} %get-tuple-element.62, f32[512,768]{0,1:T(8,128)S(1)} %get-tuple-element.63, f32[512,768]{0,1:T(8,128)S(1)} %bitcast.144), kind=kOutput, calls=%fused_computation.84 | convolution fusion | flops 3645898752 | bytes 18087936 | tf_op jit(solution)/shard_map/rd,re->de/dot_general | solution.py:204
  418.5 10.7 %fusion.43 = f32[768,3072]{1,0:T(8,128)} fusion(bf16[1024,3072]{1,0:T(8,128)(2,1)} %get-tuple-element.61, f32[1024,768]{1,0:T(8,128)S(1)} %get-tuple-element.55, f32[768]{0:T(1024)S(1)} %get-tuple-element.21, f32[768]{0:T(1024)S(1)} %get-tuple-element.26, f32[1024]{0:T(1024)S(1)} %fusion.102, f32[1024]{0:T(1024)S(1)} %broadcast_multiply_fusion.1), kind=kOutput, calls=%fused_computation.59 | convolution fusion | flops 4835770368 | bytes 18888704 | tf_op jit(solution)/shard_map/rd,rf->df/dot_general | solution.py:175
  431.2 11.0 %fusion.125 = f32[3072,768]{1,0:T(8,128)} fusion(bf16[1024,3072]{1,0:T(8,128)(2,1)} %get-tuple-element.34, f32[1024,768]{1,0:T(8,128)S(1)} %copy-done.4, f32[1024]{0:T(1024)S(1)} %negate_multiply_fusion.2), kind=kOutput, calls=%fused_computation.173 | convolution fusion | flops 4833411072 | bytes 18878464 | tf_op jit(solution)/shard_map/rf,rd->fd/dot_general | solution.py:167
  445.6 9.5 %pad_maximum_fusion = f32[1024,2304]{0,1:T(8,128)} fusion(f32[512,2304]{0,1:T(8,128)} %copy-done.1, f32[512,768]{0,1:T(8,128)} %copy-done.12, f32[512,768]{0,1:T(8,128)} %copy-done.14, f32[512,768]{0,1:T(8,128)} %bitcast.143), kind=kLoop, calls=%fused_computation.27 | loop fusion | flops 7077888 | bytes 18874368 | tf_op jit(solution)/shard_map/concatenate | solution.py:199
  458.5 40.3 %all-reduce.4 = (f32[2,768]{1,0:T(2,128)S(1)}, f32[6,768]{1,0:T(8,128)S(1)}, f32[3072]{0:T(1024)S(1)}) all-reduce(f32[2,768]{1,0:T(2,128)S(1)} %pad_maximum_fusion.9, f32[6,768]{1,0:T(8,128)S(1)} %stack.27, f32[3072]{0:T(1024)S(1)} %get-tuple-element.60), channel_id=6, replica_groups=mesh['dp'=8,'fsdp'=4] {'dp','fsdp'}, use_global_device_ids=true, to_apply=%region_20.21.clone | all-reduce | flops 9216 | bytes 73728
  503.3 8.3 %add_convert_fusion.1 = bf16[1024,768]{1,0:T(8,128)(2,1)S(1)} fusion(f32[1024,768]{1,0:T(8,128)S(1)} %copy-done.3, f32[1024]{0:T(1024)S(1)} %negate_multiply_fusion.1, bf16[768,2304]{1,0:T(8,128)(2,1)} %all-gather.7.cloned.1.call-done, f32[512,2304]{0,1:T(8,128)} %copy-done.1, f32[512,768]{0,1:T(8,128)S(1)} %copy-done.13, f32[512,768]{0,1:T(8,128)} %copy-done.14, ...), kind=kOutput, calls=%fused_computation.53 | convolution fusion | flops 3645112320 | bytes 17698816 | tf_op jit(solution)/shard_map/re,de->rd/dot_general | solution.py:209
  512.9 28.1 %reduce-scatter.7.cloned.1.call-done = f32[24,2304]{1,0:T(8,128)} async-done(((f32[768,2304]{1,0:T(8,128)}), f32[24,2304]{1,0:T(8,128)}) %reduce-scatter.7.cloned.1.call-update) | async-done | bytes 221200 | tf_op jit(solution)/shard_map/reduce_scatter | solution.py:233
  541.0 141.3 %reduce-scatter.11.cloned.1.call-done = f32[24,3072]{1,0:T(8,128)} async-done(((f32[768,3072]{1,0:T(8,128)}), f32[24,3072]{1,0:T(8,128)}) %reduce-scatter.11.cloned.1.call-update) | async-done | bytes 294928 | tf_op jit(solution)/shard_map/reduce_scatter | solution.py:235
  682.2 142.1 %reduce-scatter.13.cloned.1.call-done = f32[96,768]{1,0:T(8,128)} async-done(((f32[3072,768]{1,0:T(8,128)}), f32[96,768]{1,0:T(8,128)}) %reduce-scatter.13.cloned.1.call-update) | async-done | bytes 294928 | tf_op jit(solution)/shard_map/reduce_scatter | solution.py:236
  (159 shorter events, 72.7 us)
Async XLA Ops:
  7.2 112.7 %all-gather.7.cloned.1.call-start = ((), (), s32[]{:S(2)}) async-start(), calls=%async_computation.4 | async-start | bytes 3649536 | tf_op jit(solution)/shard_map/all_gather | solution.py:104
  7.9 150.7 %all-gather.9.cloned.1.call-start = ((), (), s32[]{:S(2)}) async-start(), calls=%async_computation.5 | async-start | bytes 1216512 | tf_op jit(solution)/shard_map/all_gather | solution.py:105
  8.7 184.5 %all-gather.11.cloned.1.call-start = ((), (), s32[]{:S(2)}) async-start(), calls=%async_computation.6 | async-start | bytes 4866048 | tf_op jit(solution)/shard_map/all_gather | solution.py:106
  9.4 249.0 %all-gather.13.cloned.1.call-start = ((), (), s32[]{:S(2)}) async-start(), calls=%async_computation.7 | async-start | bytes 4866048 | tf_op jit(solution)/shard_map/all_gather | solution.py:107
  10.0 502.9 %reduce-scatter.9.cloned.1.call-start = ((), (), s32[]{:S(2)}) async-start(), calls=%async_computation.9 | async-start | bytes 2433024 | tf_op jit(solution)/shard_map/reduce_scatter | solution.py:234
  10.7 141.8 %copy-start.29 = (pred[512]{0:T(512)(128)(4,1)}, pred[512]{0:T(512)(128)(4,1)S(1)}, u32[]{:S(2)}) copy-start(pred[512]{0:T(512)(128)(4,1)S(1)} %iota_compare_fusion) | copy-start | bytes 1540
  11.4 128.8 %copy-start.34 = (pred[4,128]{1,0:T(4,128)(4,1)}, pred[4,128]{1,0:T(4,128)(4,1)S(1)}, u32[]{:S(2)}) copy-start(pred[4,128]{1,0:T(4,128)(4,1)S(1)} %get-tuple-element.49) | copy-start | bytes 1540
  136.9 7.3 copy-start.15
  140.2 12.3 %copy-start.8 = (bf16[512,2304]{0,1:T(8,128)(2,1)}, bf16[512,2304]{0,1:T(8,128)(2,1)S(1)}, u32[]{:S(2)}) copy-start(bf16[512,2304]{0,1:T(8,128)(2,1)S(1)} %copy.90) | copy-start | bytes 7077892
  149.8 4.6 copy-start
  267.8 3.1 copy-start.27
  304.3 3.3 copy-start.23
  304.3 3.2 copy-start.33
  317.9 4.2 copy-start.24
  317.9 223.0 %reduce-scatter.7.cloned.1.call-start = ((), (), s32[]{:S(2)}) async-start(), calls=%async_computation.8 | async-start | bytes 7299072 | tf_op jit(solution)/shard_map/reduce_scatter | solution.py:233
  318.2 3.9 copy-start.7
  318.2 3.9 copy-start.9
  322.1 2.4 copy-start.35
  347.4 3.8 copy-start.22
  347.4 6.0 copy-start.21
  399.8 8.0 copy-start.12
  399.8 8.0 copy-start.14
  399.8 7.4 copy-start.19
  399.9 7.4 copy-start.20
  407.3 2.8 copy-start.10
  407.3 2.8 copy-start.31
  407.3 2.8 copy-start.32
  418.5 263.8 %reduce-scatter.11.cloned.1.call-start = ((), (), s32[]{:S(2)}) async-start(), calls=%async_computation.10 | async-start | bytes 9732096 | tf_op jit(solution)/shard_map/reduce_scatter | solution.py:235
  429.2 395.1 %reduce-scatter.13.cloned.1.call-start = ((), (), s32[]{:S(2)}) async-start(), calls=%async_computation.11 | async-start | bytes 9732096 | tf_op jit(solution)/shard_map/reduce_scatter | solution.py:236
  442.2 3.0 copy-start.5
  498.8 4.5 copy-start.11
  498.8 4.5 copy-start.13
  (12 other events, 21.8 us)
Sparse Core Ops, SparseCore 0:
  10.9 59.9 all-gather.6
  73.8 52.7 all-gather.8
  129.5 63.6 all-gather.10
  196.0 62.3 all-gather.12
  318.1 97.1 reduce-scatter.8
  422.3 118.6 reduce-scatter.6
  547.5 134.7 reduce-scatter.10
  689.7 134.5 reduce-scatter.12
where the time goes:
time: 840 us; the launch traced here: 832 us
  waiting for transfers between devices  372 us (44%)
  matrix products  219 us (26%)
  blocking collectives  145 us (17%)
  local copies, waits for them, and re-layouts  49.9 us (6%)
  other arithmetic  28.8 us (3%)
  between operations  15.9 us (2%)
    reduce_scatter x1, waiting for transfers between devices, per_device(): lax.psum_scatter(terms[3], ('dp', 'fsdp'), scatter_dimension=0, tiled=True)  142 us
    reduce_scatter x1, waiting for transfers between devices, per_device(): lax.psum_scatter(terms[2], ('dp', 'fsdp'), scatter_dimension=0, tiled=True)  141 us
    unnamed x2, blocking collectives  80.8 us
    dot_general x1, matrix products, per_device(): jnp.dot(normed_low, full_inner, preferred_element_type=jnp.float32)  35.8 us
    all_gather x1, blocking collectives, per_device(): lax.all_gather(owned[5], ('dp', 'fsdp'), axis=1, tiled=True)  33 us
    all_gather x1, blocking collectives, per_device(): lax.all_gather(owned[4], ('dp', 'fsdp'), axis=1, tiled=True)  31.6 us
    all_gather x1, waiting for transfers between devices, per_device(): lax.all_gather(owned[3], ('dp', 'fsdp'), axis=0, tiled=True)  29.4 us
    all_gather x1, waiting for transfers between devices, per_device(): lax.all_gather(owned[2], ('dp', 'fsdp'), axis=0, tiled=True)  28.8 us
  transfers between devices with their start and end apart: 8, of which 5 were waited for; matrix products, arithmetic and copies ran while one was open for 28% of the time, Pallas kernels for 0%

commit v1 on v0

v1 whole, which is shorter than its diff:
```python
import functools
import math

import jax
import jax.numpy as jnp
from jax import lax
from jax.experimental import pallas as pl
from jax.experimental.pallas import tpu as pltpu
from jax.sharding import PartitionSpec as P

HEADS = 12
EPSILON = 1e-12
MASKED = -1000000000.0
LOG2E = math.log2(math.e)
AXES = ("dp", "fsdp")
BF = jnp.bfloat16
F32 = jnp.float32
TAIL_P = 0.34
TAIL_C = (
    0.1357184499502182,
    0.13244222104549408,
    0.14697369933128357,
    -0.012965014204382896,
    0.246027871966362,
    -0.1909387707710266,
    0.04274154454469681,
)
VM = pl.BlockSpec(memory_space=pltpu.VMEM)
SM = pl.BlockSpec(memory_space=pltpu.SMEM)


def sds(shape, dtype):
    return jax.ShapeDtypeStruct(shape, dtype)


def params(mib):
    return pltpu.CompilerParams(vmem_limit_bytes=int(mib * 2**20))


def cost(flops=0, nbytes=0, trans=0):
    return pl.CostEstimate(flops=int(flops), bytes_accessed=int(nbytes), transcendentals=int(trans))


def mm(a, b):
    return lax.dot_general(a, b, (((1,), (0,)), ((), ())), preferred_element_type=F32)


def mm_nt(a, b):
    return lax.dot_general(a, b, (((1,), (1,)), ((), ())), preferred_element_type=F32)


def mm_tn(a, b):
    return lax.dot_general(a, b, (((0,), (0,)), ((), ())), preferred_element_type=F32)


class Net:
    def __init__(self, mesh):
        self.inner = mesh.shape["fsdp"]
        self.n = mesh.shape["dp"] * self.inner
        bits = self.n.bit_length() - 1
        self.core = [0, 1]
        self.xy = [0, 2, 4, 6]
        self.far = [k << 3 for k in range(self.n >> 3)]
        self.usable = self.n == 1 << bits and bits >= 4

    def index(self):
        return lax.axis_index("dp") * self.inner + lax.axis_index("fsdp")

    def swap(self, x, k):
        return lax.ppermute(x, AXES, [(i, i ^ k) for i in range(self.n)])

    def stack(self, pieces):
        k, r, c = pieces[0].shape
        m = len(pieces)

        def body(*refs):
            for i in range(m):
                refs[-1][i * k : (i + 1) * k] = refs[i][...]

        size = m * pieces[0].size * 2
        return pl.pallas_call(
            body,
            out_shape=sds((m * k, r, c), pieces[0].dtype),
            in_specs=[VM] * m,
            out_specs=VM,
            compiler_params=params(2 * size / 2**20 + 1),
            cost_estimate=cost(0, size),
        )(*pieces)

    def gather_pieces(self, block):
        far = self.stack([block] + [self.swap(block, k) for k in self.far[1:]])
        near = self.stack([far] + [self.swap(far, k) for k in self.xy[1:]])
        offs = [x ^ z for x in self.xy for z in self.far]
        return [(near, offs), (self.swap(near, 1), [o ^ 1 for o in offs])]


def place(net, pieces, parts):
    total = len(pieces)

    def body(*refs):
        idx = net.index()
        outs = refs[total:]
        for ref, (_, offs) in zip(refs, pieces):
            for j, off in enumerate(offs):
                owner = idx ^ off
                for out, (col, rows, groups, width) in zip(outs, parts):
                    for g in range(groups):
                        out[owner, g * rows : (g + 1) * rows, :] = ref[
                            j, :rows, col + g * width : col + (g + 1) * width
                        ]

    size = sum(a.size * 2 for a, _ in pieces)
    return pl.pallas_call(
        body,
        out_shape=[sds((net.n, rows * groups, width), BF) for _, rows, groups, width in parts],
        in_specs=[VM] * total,
        out_specs=[VM] * len(parts),
        compiler_params=params(2 * size / 2**20 + 1),
        cost_estimate=cost(0, size),
    )(*[a for a, _ in pieces])


def scatter_sum(net, grad):
    n, r, c = grad.shape
    offs = [x ^ z for x in net.xy for z in net.far]
    nz = len(net.far)
    idx_of = net.index

    def first(g, out):
        idx = idx_of()
        for j, off in enumerate(offs):
            out[j] = g[idx ^ off ^ 1].astype(BF)

    half = len(offs) * r * c
    send = pl.pallas_call(
        first,
        out_shape=sds((len(offs), r, c), BF),
        in_specs=[VM],
        out_specs=VM,
        compiler_params=params((half * 12 + half * 0) / 2**20 + 1),
        cost_estimate=cost(0, half * 6),
    )(grad)
    got = net.swap(send, 1)

    def second(g, a, *outs):
        idx = idx_of()
        for o, out in enumerate(outs):
            for z in range(nz):
                j = (o + 1) * nz + z
                out[z] = (g[idx ^ offs[j]] + a[j].astype(F32)).astype(BF)

    sends = pl.pallas_call(
        second,
        out_shape=[sds((nz, r, c), BF)] * 3,
        in_specs=[VM, VM],
        out_specs=[VM] * 3,
        compiler_params=params(half * 14 / 2**20 + 1),
        cost_estimate=cost(0, half * 6),
    )(grad, got)
    got2 = [net.swap(s, k) for s, k in zip(sends, net.xy[1:])]

    def third(g, a, b0, b1, b2, own, *outs):
        idx = idx_of()
        for z in range(nz):
            t = g[idx ^ offs[z]] + a[z].astype(F32)
            t = t + b0[z].astype(F32) + b1[z].astype(F32) + b2[z].astype(F32)
            if z == 0:
                own[...] = t
            else:
                outs[z - 1][0] = t.astype(BF)

    res = pl.pallas_call(
        third,
        out_shape=[sds((r, c), F32)] + [sds((1, r, c), BF)] * (nz - 1),
        in_specs=[VM] * 5,
        out_specs=[VM] * nz,
        compiler_params=params(half * 14 / 2**20 + 1),
        cost_estimate=cost(0, half * 3),
    )(grad, got, *got2)
    total = res[0]
    for s, k in zip(res[1:], net.far[1:]):
        total = total + net.swap(s, k)[0].astype(F32)
    return total


class Shape:
    def __init__(self, queries, qlen, passages, plen):
        self.rq = queries * qlen
        self.rp = passages * plen
        self.rows = self.rq + self.rp
        self.segs = [(i * qlen, qlen, 0, i) for i in range(queries)]
        self.segs += [(self.rq + i * plen, plen, 1, i) for i in range(passages)]
        self.block = math.gcd(256, math.gcd(self.rq, self.rp))
        self.steps = self.rows // self.block
        self.nq = self.rq // self.block

    def valid(self, i, lens):
        row = lax.broadcasted_iota(jnp.int32, (self.block, 1), 0) + i * self.block
        ok = None
        for base, _, which, k in self.segs:
            here = (row >= base) & (row < base + lens[which][k])
            ok = here if ok is None else ok | here
        return ok

    def both(self, width):
        b, nq = self.block, self.nq
        return [
            pl.BlockSpec((b, width), lambda i, *_: (jnp.minimum(i, nq - 1), 0)),
            pl.BlockSpec((b, width), lambda i, *_: (jnp.maximum(i - nq, 0), 0)),
        ]

    def rowspec(self, width):
        return pl.BlockSpec((self.block, width), lambda i, *_: (i, 0))


def once(shape):
    return pl.BlockSpec(shape, lambda i, *_: (0,) * len(shape))


def qkv_project(sh, xq, xp, w, shift):
    d = xq.shape[1]
    width = shift.shape[1]

    def body(xq, xp, w, b, o):
        i = pl.program_id(0)
        x = jnp.where(i < sh.nq, xq[...], xp[...])
        for c in range(0, width, d):
            o[:, c : c + d] = (mm(x, w[:, c : c + d]) + b[:, c : c + d]).astype(BF)

    return pl.pallas_call(
        body,
        grid=(sh.steps,),
        out_shape=sds((sh.rows, width), BF),
        in_specs=sh.both(d) + [VM, VM],
        out_specs=sh.rowspec(width),
        compiler_params=params(24),
        cost_estimate=cost(2 * sh.rows * d * width, sh.rows * (d + width) * 2),
    )(xq, xp, w, shift)


def attend(sh, lens, qkv):
    d = qkv.shape[1] // 3
    hd = d // HEADS
    pw = 2 * hd
    pairs = HEADS // 2

    def body(ql, pln, q, k, v, ctx, lse):
        lane = lax.broadcasted_iota(jnp.int32, (1, pw), 1)
        for base, ln, which, i in sh.segs:
            n = (ql, pln)[which][i]
            rows = slice(base, base + ln)
            qb, kb, vb = q[rows, :], k[rows, :], v[rows, :]
            vt = vb.T
            keep = lax.broadcasted_iota(jnp.int32, (ln, 1), 0) < n
            outs = []
            for h in range(2):
                kh = jnp.where((lane >= h * hd) & (lane < (h + 1) * hd), kb, jnp.zeros_like(kb))
                s = mm_nt(kh, qb) * (0.125 * LOG2E)
                s = jnp.where(keep, s, MASKED * LOG2E)
                top = jnp.max(s, axis=0, keepdims=True)
                e = jnp.exp2(s - top)
                tot = jnp.sum(e, axis=0, keepdims=True)
                outs.append(mm(vt[h * hd : (h + 1) * hd], e.astype(BF)) * (1.0 / tot))
                lse[0, h : h + 1, rows] = top + jnp.log(tot) * LOG2E
            ctx[rows, :] = jnp.concatenate(outs, axis=0).T.astype(BF)

    def col(c):
        return pl.BlockSpec((sh.rows, pw), lambda j, *_: (0, c * pairs + j))

    grid_spec = pltpu.PrefetchScalarGridSpec(
        num_scalar_prefetch=2,
        grid=(pairs,),
        in_specs=[col(0), col(1), col(2)],
        out_specs=[col(0), pl.BlockSpec((1, 2, sh.rows), lambda j, *_: (j, 0, 0))],
    )
    sq = sum(ln * ln for _, ln, _, _ in sh.segs)
    return pl.pallas_call(
        body,
        grid_spec=grid_spec,
        out_shape=[sds((sh.rows, d), BF), sds((pairs, 2, sh.rows), F32)],
        compiler_params=params(24),
        cost_estimate=cost(4 * 4 * sq * d, sh.rows * d * 8, sq * HEADS),
    )(*lens, qkv, qkv, qkv)


def attend_back(sh, lens, qkv, ctx, dctx, lse):
    d = qkv.shape[1] // 3
    hd = d // HEADS
    pw = 2 * hd
    pairs = HEADS // 2

    def body(ql, pln, q, k, v, c, dc, lse, dq, dk, dv, sums):
        lane = lax.broadcasted_iota(jnp.int32, (1, pw), 1)
        sum_q = jnp.zeros((1, pw), F32)
        sum_v = jnp.zeros((1, pw), F32)
        for base, ln, which, i in sh.segs:
            n = (ql, pln)[which][i]
            rows = slice(base, base + ln)
            qb, kb, vb, dcb = q[rows, :], k[rows, :], v[rows, :], dc[rows, :]
            kt = kb.T
            prod = (dcb.astype(F32) * c[rows, :].astype(F32)).T
            keep = lax.broadcasted_iota(jnp.int32, (ln, 1), 0) < n
            dqs, dva, dka = [], None, None
            for h in range(2):
                mine = (lane >= h * hd) & (lane < (h + 1) * hd)
                zero = jnp.zeros_like(kb)
                kh = jnp.where(mine, kb, zero)
                qh = jnp.where(mine, qb, zero)
                dch = jnp.where(mine, dcb, zero)
                s = mm_nt(kh, qb) * (0.125 * LOG2E)
                s = jnp.where(keep, s, MASKED * LOG2E)
                p = jnp.exp2(s - lse[0, h : h + 1, rows])
                across = jnp.sum(prod[h * hd : (h + 1) * hd], axis=0, keepdims=True)
                ds = (p * (mm_nt(vb, dch) - across)).astype(BF)
                one_v = mm(p.astype(BF), dch)
                one_k = mm(ds, qh)
                dva = one_v if dva is None else dva + one_v
                dka = one_k if dka is None else dka + one_k
                dqs.append(mm(kt[h * hd : (h + 1) * hd], ds))
            dqa = jnp.concatenate(dqs, axis=0).T * 0.125
            dq[rows, :] = dqa.astype(BF)
            dk[rows, :] = (dka * 0.125).astype(BF)
            dv[rows, :] = dva.astype(BF)
            sum_q = sum_q + jnp.sum(dqa, axis=0, keepdims=True)
            sum_v = sum_v + jnp.sum(dva, axis=0, keepdims=True)
        sums[0:1, :] = sum_q
        sums[1:2, :] = sum_v

    def col(c):
        return pl.BlockSpec((sh.rows, pw), lambda j, *_: (0, c * pairs + j))

    grid_spec = pltpu.PrefetchScalarGridSpec(
        num_scalar_prefetch=2,
        grid=(pairs,),
        in_specs=[col(0), col(1), col(2), col(0), col(0)]
        + [pl.BlockSpec((1, 2, sh.rows), lambda j, *_: (j, 0, 0))],
        out_specs=[col(0)] * 3 + [pl.BlockSpec((2, pw), lambda j, *_: (0, j))],
    )
    sq = sum(ln * ln for _, ln, _, _ in sh.segs)
    return pl.pallas_call(
        body,
        grid_spec=grid_spec,
        out_shape=[sds((sh.rows, d), BF)] * 3 + [sds((2, d), F32)],
        compiler_params=params(32),
        cost_estimate=cost(4 * 10 * sq * d, sh.rows * d * 16, sq * HEADS),
    )(*lens, qkv, qkv, qkv, ctx, dctx, lse)


def first_norm(sh, ctx, xq, xp, w, small):
    d = ctx.shape[1]

    def body(c, xq, xp, w, sm, hat, scale, low):
        i = pl.program_id(0)
        x = jnp.where(i < sh.nq, xq[...], xp[...]).astype(F32)
        h = x + mm(c[...], w[...]) + sm[4:5, :]
        h = h - jnp.mean(h, axis=-1, keepdims=True)
        r = lax.rsqrt(jnp.mean(h * h, axis=-1, keepdims=True) + EPSILON)
        xhat = h * r
        hat[...] = xhat
        scale[...] = r
        low[...] = (xhat * sm[0:1, :] + sm[5:6, :]).astype(BF)

    return pl.pallas_call(
        body,
        grid=(sh.steps,),
        out_shape=[sds((sh.rows, d), F32), sds((sh.rows, 1), F32), sds((sh.rows, d), BF)],
        in_specs=[sh.rowspec(d)] + sh.both(d) + [VM, VM],
        out_specs=[sh.rowspec(d), sh.rowspec(1), sh.rowspec(d)],
        compiler_params=params(20),
        cost_estimate=cost(2 * sh.rows * d * d, sh.rows * d * 10),
    )(ctx, xq, xp, w, small)


def upward(sh, low, w, bias):
    d = low.shape[1]
    ff = w.shape[1]
    step = math.gcd(ff, 512)

    def body(low, w, b, act, slope):
        x = low[...]
        for c in range(0, ff, step):
            cols = slice(c, c + step)
            u = mm(x, w[:, cols]) + b[:, cols]
            t = 1.0 / (1.0 + TAIL_P * jnp.abs(u))
            poly = jnp.full_like(t, TAIL_C[-1])
            for co in TAIL_C[-2::-1]:
                poly = poly * t + co
            bell = jnp.exp2((u * u) * (-0.5 * LOG2E))
            tail = poly * t * bell
            phi = jnp.where(u > 0, 1.0 - tail, tail)
            act[:, cols] = (u * phi).astype(BF)
            slope[:, cols] = (phi + (u * (1.0 / math.sqrt(2.0 * math.pi))) * bell).astype(BF)

    return pl.pallas_call(
        body,
        grid=(sh.steps,),
        out_shape=[sds((sh.rows, ff), BF)] * 2,
        in_specs=[sh.rowspec(d), VM, VM],
        out_specs=[sh.rowspec(ff)] * 2,
        compiler_params=params(28),
        cost_estimate=cost(2 * sh.rows * d * ff, sh.rows * ff * 4, sh.rows * ff * 8),
    )(low, w, bias)


def second_norm(sh, lens, act, hat, cq, cp, w, small):
    d = hat.shape[1]
    ff = act.shape[1]

    def body(ql, pln, act, hat, cq, cp, w, sm, oq, op, dh, low, sums):
        i = pl.program_id(0)
        ok = sh.valid(i, (ql, pln))
        h = hat[...] * sm[0:1, :] + sm[5:6, :] + (mm(act[...], w[...]) + sm[6:7, :])
        h = h - jnp.mean(h, axis=-1, keepdims=True)
        r = lax.rsqrt(jnp.mean(h * h, axis=-1, keepdims=True) + EPSILON)
        xhat = h * r
        out = jnp.where(ok, xhat * sm[1:2, :] + sm[7:8, :], 0.0).astype(BF)

        @pl.when(i < sh.nq)
        def _():
            oq[...] = out

        @pl.when(i >= sh.nq)
        def _():
            op[...] = out

        dy = jnp.where(ok, jnp.where(i < sh.nq, cq[...], cp[...]).astype(F32), 0.0)
        t = dy * sm[1:2, :]
        prod = jnp.mean(t * xhat, axis=-1, keepdims=True)
        g = r * (t - jnp.mean(t, axis=-1, keepdims=True) - xhat * prod)
        dh[...] = g
        low[...] = g.astype(BF)
        rows = jnp.concatenate(
            [jnp.sum(z, axis=0, keepdims=True) for z in (dy * xhat, dy, g)], axis=0
        )

        @pl.when(i == 0)
        def _():
            sums[...] = rows

        @pl.when(i > 0)
        def _():
            sums[...] += rows

    grid_spec = pltpu.PrefetchScalarGridSpec(
        num_scalar_prefetch=2,
        grid=(sh.steps,),
        in_specs=[sh.rowspec(ff), sh.rowspec(d)] + sh.both(d) + [VM, VM],
        out_specs=sh.both(d) + [sh.rowspec(d), sh.rowspec(d), once((3, d))],
    )
    return pl.pallas_call(
        body,
        grid_spec=grid_spec,
        out_shape=[
            sds((sh.rq, d), BF),
            sds((sh.rp, d), BF),
            sds((sh.rows, d), F32),
            sds((sh.rows, d), BF),
            sds((3, d), F32),
        ],
        compiler_params=params(28),
        cost_estimate=cost(2 * sh.rows * d * ff, sh.rows * (ff * 2 + d * 14)),
    )(*lens, act, hat, cq, cp, w, small)


def up_back(sh, low, slope, w):
    d = low.shape[1]
    ff = w.shape[0]
    step = math.gcd(ff, 512)

    def body(low, slope, w, du, sums):
        i = pl.program_id(0)
        g = low[...]
        for c in range(0, ff, step):
            cols = slice(c, c + step)
            one = mm_nt(g, w[cols, :]) * slope[:, cols].astype(F32)
            du[:, cols] = one.astype(BF)
            row = jnp.sum(one, axis=0, keepdims=True)

            @pl.when(i == 0)
            def _():
                sums[:, cols] = row

            @pl.when(i > 0)
            def _():
                sums[:, cols] += row

    return pl.pallas_call(
        body,
        grid=(sh.steps,),
        out_shape=[sds((sh.rows, ff), BF), sds((1, ff), F32)],
        in_specs=[sh.rowspec(d), sh.rowspec(ff), VM],
        out_specs=[sh.rowspec(ff), once((1, ff))],
        compiler_params=params(24),
        cost_estimate=cost(2 * sh.rows * d * ff, sh.rows * ff * 4),
    )(low, slope, w)


def first_back(sh, du, dh2, hat, scale, wi, wo, small):
    d = hat.shape[1]
    ff = du.shape[1]

    def body(du, dh2, hat, r, wi, wo, sm, dh1, low, dctx, sums):
        i = pl.program_id(0)
        dn = dh2[...] + mm_nt(du[...], wi[...])
        xhat = hat[...]
        t = dn * sm[0:1, :]
        prod = jnp.mean(t * xhat, axis=-1, keepdims=True)
        g = r[...] * (t - jnp.mean(t, axis=-1, keepdims=True) - xhat * prod)
        glow = g.astype(BF)
        dh1[...] = g
        low[...] = glow
        dctx[...] = mm_nt(glow, wo[...]).astype(BF)
        rows = jnp.concatenate(
            [jnp.sum(z, axis=0, keepdims=True) for z in (dn * xhat, dn, g)], axis=0
        )

        @pl.when(i == 0)
        def _():
            sums[...] = rows

        @pl.when(i > 0)
        def _():
            sums[...] += rows

    return pl.pallas_call(
        body,
        grid=(sh.steps,),
        out_shape=[
            sds((sh.rows, d), F32),
            sds((sh.rows, d), BF),
            sds((sh.rows, d), BF),
            sds((3, d), F32),
        ],
        in_specs=[sh.rowspec(ff), sh.rowspec(d), sh.rowspec(d), sh.rowspec(1), VM, VM, VM],
        out_specs=[sh.rowspec(d)] * 3 + [once((3, d))],
        compiler_params=params(32),
        cost_estimate=cost(2 * sh.rows * d * (ff + d), sh.rows * (ff * 2 + d * 16)),
    )(du, dh2, hat, scale, wi, wo, small)


def weight_grad(lefts, rights):
    rows = [a.shape[0] for a in lefts]
    k = lefts[0].shape[1]
    widths = [b.shape[1] for b in rights]
    width = sum(widths)
    step = 256
    cut = 768
    total = sum(rows)

    def body(*refs):
        ls, rs, out = refs[: len(lefts)], refs[len(lefts) : -1], refs[-1]
        at = 0
        for b, w in zip(rs, widths):
            for c in range(0, w, cut):
                acc, base = None, 0
                for a, r in zip(ls, rows):
                    one = mm_tn(a[...], b[base : base + r, c : c + cut])
                    acc = one if acc is None else acc + one
                    base += r
                out[:, at + c : at + c + cut] = acc
            at += w

    return pl.pallas_call(
        body,
        grid=(k // step,),
        out_shape=sds((k, width), F32),
        in_specs=[pl.BlockSpec((r, step), lambda i: (0, i)) for r in rows] + [VM] * len(rights),
        out_specs=pl.BlockSpec((step, width), lambda i: (i, 0)),
        compiler_params=params(24),
        cost_estimate=cost(2 * total * k * width, total * (k + width) * 2 + k * width * 4),
    )(*lefts, *rights)


def input_grad(sh, dh1, parts, w):
    d = dh1.shape[1]

    def body(dh1, a, b, c, w, oq, op):
        i = pl.program_id(0)
        acc = dh1[...]
        for j, part in enumerate((a, b, c)):
            acc = acc + mm_nt(part[...], w[:, j * d : (j + 1) * d])
        out = acc.astype(BF)

        @pl.when(i < sh.nq)
        def _():
            oq[...] = out

        @pl.when(i >= sh.nq)
        def _():
            op[...] = out

    return pl.pallas_call(
        body,
        grid=(sh.steps,),
        out_shape=[sds((sh.rq, d), BF), sds((sh.rp, d), BF)],
        in_specs=[sh.rowspec(d)] * 4 + [VM],
        out_specs=sh.both(d),
        compiler_params=params(24),
        cost_estimate=cost(2 * sh.rows * d * 3 * d, sh.rows * d * 12),
    )(dh1, *parts, w)


def per_device(net, *args):
    xq3, xp3, ql, pln, cq3, cp3, w_qkv, w_out, w_inner, w_outer, gains, biases, inner_bias = args
    sh = Shape(xq3.shape[0], xq3.shape[1], xp3.shape[0], xp3.shape[1])
    lens = (ql, pln)
    d = xq3.shape[2]
    n = net.n
    own = d // n
    xq, xp = xq3.reshape(sh.rq, d), xp3.reshape(sh.rp, d)
    cq, cp = cq3.reshape(sh.rq, d), cp3.reshape(sh.rp, d)
    ff = inner_bias.shape[0] * n
    groups = ff // d
    custom = net.usable and own % 8 == 0 and ff // n <= 128 and own >= 9

    full_inner = lax.all_gather(w_inner, AXES, axis=0, tiled=True)
    if custom:
        tiny = jnp.zeros((own, 128), BF)
        tiny = lax.dynamic_update_slice(tiny, gains, (0, 0))
        tiny = lax.dynamic_update_slice(tiny, biases, (2, 0))
        tiny = lax.dynamic_update_slice(tiny, inner_bias[None], (8, 0))
        head = jnp.concatenate([w_qkv, tiny], axis=1)[None]
        pieces = net.gather_pieces(head)
        full_qkv, full_tiny = place(net, pieces, [(0, own, 1, 3 * d), (3 * d, own, 1, 128)])
        full_qkv = full_qkv.reshape(d, 3 * d)
        rest = jnp.concatenate(
            [w_out] + [w_outer[g * own : (g + 1) * own] for g in range(groups)], axis=1
        )[None]
        pieces = net.gather_pieces(rest)
        full_out, full_outer = place(net, pieces, [(0, own, 1, d), (d, own, groups, d)])
        full_out, full_outer = full_out.reshape(d, d), full_outer.reshape(ff, d)
        small = full_tiny[:, :8, :own].transpose(1, 0, 2).reshape(8, d).astype(F32)
        inner_shift = full_tiny[:, 8, : ff // n].reshape(1, ff).astype(F32)
    else:
        full_qkv = lax.all_gather(w_qkv, AXES, axis=0, tiled=True)
        full_out = lax.all_gather(w_out, AXES, axis=0, tiled=True)
        full_outer = lax.all_gather(w_outer, AXES, axis=0, tiled=True)
        small = lax.all_gather(jnp.concatenate([gains, biases], 0), AXES, axis=1, tiled=True).astype(F32)
        inner_shift = lax.all_gather(inner_bias, AXES, axis=0, tiled=True)[None].astype(F32)
    qkv_shift = jnp.concatenate([small[2:3], jnp.zeros((1, d), F32), small[3:4]], axis=1)

    qkv = qkv_project(sh, xq, xp, full_qkv, qkv_shift)
    ctx, lse = attend(sh, lens, qkv)
    hat1, scale1, low1 = first_norm(sh, ctx, xq, xp, full_out, small)
    act, slope = upward(sh, low1, full_inner, inner_shift)
    out_q, out_p, dh2, low2, sums2 = second_norm(sh, lens, act, hat1, cq, cp, full_outer, small)
    g_outer = weight_grad([act], [low2])
    du, sum_du = up_back(sh, low2, slope, full_outer)
    g_inner = weight_grad([low1], [du])
    dh1, low_a, dctx, sums1 = first_back(sh, du, dh2, hat1, scale1, full_inner, full_out, small)
    g_out = weight_grad([ctx], [low_a])
    dq, dk, dv, sums_qv = attend_back(sh, lens, qkv, ctx, dctx, lse)
    g_qkv = weight_grad([xq, xp], [dq, dk, dv])
    grad_q, grad_p = input_grad(sh, dh1, (dq, dk, dv), full_qkv)
    sums = jnp.concatenate(
        [sums1[0:1], sums2[0:1], sums_qv, sums1[2:3], sums1[1:2], sums2[2:3], sums2[1:2]], axis=0
    )
    if custom:
        r_outer = scatter_sum(net, g_outer.reshape(n, ff // n, d))
        r_inner = scatter_sum(net, g_inner.reshape(n, own, ff))
        r_out = scatter_sum(net, g_out.reshape(n, own, d))
        tiny = jnp.pad(sums.reshape(8, n, own).transpose(1, 0, 2), ((0, 0), (0, 0), (0, 128 - own)))
        tail = jnp.pad(sum_du.reshape(n, 1, ff // n), ((0, 0), (0, own - 9), (0, 128 - ff // n)))
        tiny = jnp.concatenate([tiny, tail], axis=1)
        both = jnp.concatenate([g_qkv.reshape(n, own, 3 * d), tiny], axis=2)
        r_both = scatter_sum(net, both)
        r_qkv, r_tiny = r_both[:, : 3 * d], r_both[:, 3 * d :]
        r_gains, r_biases, r_ib = r_tiny[:2, :own], r_tiny[2:8, :own], r_tiny[8, : ff // n]
    else:
        def rs(x, dim=0):
            return lax.psum_scatter(x, AXES, scatter_dimension=dim, tiled=True)

        r_outer, r_inner, r_out, r_qkv = rs(g_outer), rs(g_inner), rs(g_out), rs(g_qkv)
        r_sums = rs(sums, 1)
        r_gains, r_biases, r_ib = r_sums[:2], r_sums[2:], rs(sum_du[0])
    return (
        out_q.reshape(xq3.shape),
        out_p.reshape(xp3.shape),
        grad_q.reshape(xq3.shape),
        grad_p.reshape(xp3.shape),
        r_qkv,
        r_out,
        r_inner,
        r_outer,
        r_gains,
        r_biases,
        r_ib,
    )


def solution(mesh):
    rows3, rows2, row = P(AXES, None, None), P(AXES, None), P(AXES)
    cols = P(None, AXES)
    net = Net(mesh)
    return jax.shard_map(
        functools.partial(per_device, net),
        mesh=mesh,
        in_specs=(rows3, rows3, row, row, rows3, rows3, rows2, rows2, rows2, rows2, cols, cols, row),
        out_specs=(rows3, rows3, rows3, rows3, rows2, rows2, rows2, rows2, cols, cols, row),
        check_vma=False,
    )
```

time: 840 us -> 404 us (0.48)
  waiting for transfers between devices: 372 us -> 133 us
  matrix products: 219 us -> 0 us
  blocking collectives: 145 us -> 0 us
  Pallas kernels: 0 us -> 134 us
  starting transfers between devices: 0.49 us -> 49.7 us
  other arithmetic: 28.8 us -> 5.32 us
  local copies, waits for them, and re-layouts: 49.9 us -> 61.8 us
    reduce_scatter x4 -> x0, waiting for transfers between devices: 311 us -> none  [the longest x1 142 us: per_device(): lax.psum_scatter(terms[3], ('dp', 'fsdp'), scatter_dimension=0, tiled=True)]
    dot_general x24 -> x0, matrix products: 219 us -> none  [the longest x1 35.8 us: per_device(): jnp.dot(normed_low, full_inner, preferred_element_type=jnp.float32)]
    pallas_call x0 -> x31, Pallas kernels: none -> 134 us  [the longest x1 21.9 us: attend_back(): pl.pallas_call(body, grid_spec=grid_spec, out_shape=[sds((sh.rows, d), BF...]
    ppermute x0 -> x42, waiting for transfers between devices: none -> 132 us  [swap(): return lax.ppermute(x, AXES, [(i, i ^ k) for i in range(self.n)])]
    unnamed x2 -> x0, blocking collectives: 80.8 us -> none
    all_gather x2 -> x0, blocking collectives: 64.6 us -> none  [the longest x1 33 us: per_device(): lax.all_gather(owned[5], ('dp', 'fsdp'), axis=1, tiled=True)]
    all_gather x4 -> x1, waiting for transfers between devices: 58.3 us -> 0.01 us  [per_device(): full_inner = lax.all_gather(w_inner, AXES, axis=0, tiled=True)]
    ppermute x0 -> x42, starting transfers between devices: none -> 49.6 us  [swap(): return lax.ppermute(x, AXES, [(i, i ^ k) for i in range(self.n)])]
  transfers between devices with their start and end apart: 8 -> 43, of which waited for: 5 -> 19; matrix products, arithmetic and copies ran while one was open for 28% -> 3% of each run, Pallas kernels for 0% -> 14%
where the time goes in v1:
time: 404 us; the launch traced here: 399 us
  Pallas kernels  134 us (33%)
  waiting for transfers between devices  133 us (33%)
  local copies, waits for them, and re-layouts  61.8 us (15%)
  starting transfers between devices  49.7 us (12%)
  between operations  15.4 us (4%)
  other arithmetic  5.32 us (1%)
    ppermute x42, waiting for transfers between devices, swap(): return lax.ppermute(x, AXES, [(i, i ^ k) for i in range(self.n)])  132 us
    unnamed x140, local copies, waits for them, and re-layouts  54.3 us
    ppermute x42, starting transfers between devices, swap(): return lax.ppermute(x, AXES, [(i, i ^ k) for i in range(self.n)])  49.6 us
    pallas_call x1, Pallas kernels, attend_back(): pl.pallas_call(body, grid_spec=grid_spec, out_shape=[sds((sh.rows, d), BF...  21.9 us
    pallas_call x4, Pallas kernels, weight_grad(): pl.pallas_call(body, grid=(k // step,), out_shape=sds((k, width), F32), i...  20.4 us
    pallas_call x1, Pallas kernels, attend(): pl.pallas_call(body, grid_spec=grid_spec, out_shape=[sds((sh.rows, d), BF...  17.7 us
    pallas_call x1, Pallas kernels, upward(): pl.pallas_call(body, grid=(sh.steps,), out_shape=[sds((sh.rows, ff), BF)]...  16.8 us
    pallas_call x1, Pallas kernels, first_back(): pl.pallas_call(body, grid=(sh.steps,), out_shape=[sds((sh.rows, d), F32),...  12.3 us
  transfers between devices with their start and end apart: 43, of which 19 were waited for; matrix products, arithmetic and copies ran while one was open for 3% of the time, Pallas kernels for 14%

profile of v1, /device:TPU:16, one launch (start us, length us, event | category | flops | bytes accessed | tf_op | source)
XLA Modules:
  0.0 398.5 jit_solution(12975406052373253006)
XLA Ops:
  18.5 4.5 %collective-permute-done.1.refs_2_ = bf16[1,24,2432]{2,1,0:T(8,128)(2,1)S(1)} collective-permute-done((bf16[1,24,2432]{2,1,0:T(8,128)(2,1)S(1)}, bf16[1,24,2432]{2,1,0:T(8,128)(2,1)S(1)}, u32[]{:S(2)}, u32[]{:S(2)}) %collective-permute-start.1) | collective-permute-done | bytes 116768 | tf_op jit(solution)/shard_map/ppermute | solution.py:70
  22.9 4.1 %collective-permute-done.2.refs_3_ = bf16[1,24,2432]{2,1,0:T(8,128)(2,1)S(1)} collective-permute-done((bf16[1,24,2432]{2,1,0:T(8,128)(2,1)S(1)}, bf16[1,24,2432]{2,1,0:T(8,128)(2,1)S(1)}, u32[]{:S(2)}, u32[]{:S(2)}) %collective-permute-start.2) | collective-permute-done | bytes 116768 | tf_op jit(solution)/shard_map/ppermute | solution.py:70
  38.5 8.4 %collective-permute-done.8.refs_2_ = bf16[1,24,3840]{2,1,0:T(8,128)(2,1)S(1)} collective-permute-done((bf16[1,24,3840]{2,1,0:T(8,128)(2,1)S(1)}, bf16[1,24,3840]{2,1,0:T(8,128)(2,1)S(1)}, u32[]{:S(2)}, u32[]{:S(2)}) %collective-permute-start.8) | collective-permute-done | bytes 184352 | tf_op jit(solution)/shard_map/ppermute | solution.py:70
  46.9 6.5 %collective-permute-done.9.refs_3_ = bf16[1,24,3840]{2,1,0:T(8,128)(2,1)S(1)} collective-permute-done((bf16[1,24,3840]{2,1,0:T(8,128)(2,1)S(1)}, bf16[1,24,3840]{2,1,0:T(8,128)(2,1)S(1)}, u32[]{:S(2)}, u32[]{:S(2)}) %collective-permute-start.9) | collective-permute-done | bytes 184352 | tf_op jit(solution)/shard_map/ppermute | solution.py:70
  57.1 3.7 collective-permute-done.5.refs_3_
  61.0 24.0 %collective-permute-done.10.refs_1_ = bf16[4,24,3840]{2,1,0:T(8,128)(2,1)S(1)} collective-permute-done((bf16[4,24,3840]{2,1,0:T(8,128)(2,1)S(1)}, bf16[4,24,3840]{2,1,0:T(8,128)(2,1)S(1)}, u32[]{:S(2)}, u32[]{:S(2)}) %collective-permute-start.10) | collective-permute-done | bytes 737312 | tf_op jit(solution)/shard_map/ppermute | solution.py:70
  85.1 11.9 %collective-permute-done.12.refs_3_ = bf16[4,24,3840]{2,1,0:T(8,128)(2,1)S(1)} collective-permute-done((bf16[4,24,3840]{2,1,0:T(8,128)(2,1)S(1)}, bf16[4,24,3840]{2,1,0:T(8,128)(2,1)S(1)}, u32[]{:S(2)}, u32[]{:S(2)}) %collective-permute-start.12) | collective-permute-done | bytes 737312 | tf_op jit(solution)/shard_map/ppermute | solution.py:70
  104.9 4.4 %shard_map.215.q.k.v = bf16[1024,2304]{1,0:T(8,128)(2,1)S(1)} custom-call(bf16[512,768]{1,0:T(8,128)(2,1)S(1)} %bitcast.88, bf16[512,768]{1,0:T(8,128)(2,1)S(1)} %bitcast.91, bf16[768,2304]{1,0:T(8,128)(2,1)S(1)} %bitcast.82, f32[1,2304]{1,0:T(1,128)S(1)} %fusion.3.b), custom_call_target="tpu_custom_call" | custom-call | flops 3623878656 | bytes 6291456 | tf_op jit(solution)/shard_map/pallas_call | solution.py:230
  109.3 17.7 %shard_map.216 = (bf16[1024,768]{1,0:T(8,128)(2,1)S(1)}, f32[6,2,1024]{2,1,0:T(2,128)S(1)}) custom-call(s32[4]{0:T(128)S(1)} %copy-done.31, s32[1]{0:T(128)S(6)} %copy.35.pln, bf16[1024,2304]{1,0:T(8,128)(2,1)S(1)} %shard_map.215.q.k.v, bf16[1024,2304]{1,0:T(8,128)(2,1)S(1)} %shard_map.215.q.k.v, bf16[1024,2304]{1,0:T(8,128)(2,1)S(1)} %shard_map.215.q.k.v), custom_call_target="tpu_custom_call" | custom-call | flops 4026531840 | bytes 6291456 | tf_op jit(solution)/shard_map/pallas_call | solution.py:277
  134.3 2.9 shard_map.220
  145.6 16.8 %shard_map.221 = (bf16[1024,3072]{1,0:T(8,128)(2,1)S(1)}, bf16[1024,3072]{1,0:T(8,128)(2,1)S(1)}) custom-call(bf16[1024,768]{1,0:T(8,128)(2,1)S(1)} %copy-done.44, bf16[768,3072]{1,0:T(8,128)(2,1)S(1)} %copy-done.10, f32[1,3072]{1,0:T(1,128)S(1)} %reshape.132.b), custom_call_target="tpu_custom_call" | custom-call | flops 4831838208 | bytes 12582912 | tf_op jit(solution)/shard_map/pallas_call | solution.py:394
  162.4 10.6 %shard_map.222 = (bf16[512,768]{1,0:T(8,128)(2,1)}, bf16[512,768]{1,0:T(8,128)(2,1)}, f32[1024,768]{1,0:T(8,128)S(1)}, bf16[1024,768]{1,0:T(8,128)(2,1)S(1)}, f32[3,768]{1,0:T(4,128)S(1)}) custom-call(s32[4]{0:T(128)S(1)} %copy-done.31, s32[1]{0:T(128)S(6)} %copy.35.pln, bf16[1024,3072]{1,0:T(8,128)(2,1)S(1)} %get-tuple-element.72.act.refs_0_, ...), custom_call_target="tpu_custom_call" | custom-call | flops 4831838208 | bytes 17301504 | tf_op jit(solution)/shard_map/pallas_call | solution.py:450
  174.8 10.0 %shard_map.223 = (bf16[1024,3072]{1,0:T(8,128)(2,1)S(1)}, f32[1,3072]{1,0:T(1,128)S(1)}) custom-call(bf16[1024,768]{1,0:T(8,128)(2,1)S(1)} %get-tuple-element.77.low.refs_1_, bf16[1024,3072]{1,0:T(8,128)(2,1)S(1)} %get-tuple-element.78.slope, bf16[3072,768]{1,0:T(8,128)(2,1)S(1)} %bitcast.81), custom_call_target="tpu_custom_call" | custom-call | flops 4831838208 | bytes 12582912 | tf_op jit(solution)/shard_map/pallas_call | solution.py:487
  191.6 5.6 %shard_map.235 = f32[768,3072]{1,0:T(8,128)S(1)} custom-call(bf16[1024,768]{1,0:T(8,128)(2,1)S(1)} %copy-done.45, bf16[1024,3072]{1,0:T(8,128)(2,1)S(1)} %copy-done.50), custom_call_target="tpu_custom_call" | custom-call | flops 4831838208 | bytes 17301504 | tf_op jit(solution)/shard_map/pallas_call | solution.py:563
  197.2 3.5 copy-done
  203.1 12.3 %shard_map.224 = (f32[1024,768]{1,0:T(8,128)S(1)}, bf16[1024,768]{1,0:T(8,128)(2,1)S(1)}, bf16[1024,768]{1,0:T(8,128)(2,1)S(1)}, f32[3,768]{1,0:T(4,128)S(1)}) custom-call(bf16[1024,3072]{1,0:T(8,128)(2,1)} %copy-done.49, f32[1024,768]{1,0:T(8,128)S(1)} %copy-done.57, f32[1024,768]{1,0:T(8,128)S(1)} %copy-done.42, f32[1024,1]{1,0:T(8,128)S(1)} %copy-done.47, ...), custom_call_target="tpu_custom_call" | custom-call | flops 6039797760 | bytes 18874368 | tf_op jit(solution)/shard_map/pallas_call | solution.py:525
  215.4 21.9 %shard_map.225 = (bf16[1024,768]{1,0:T(8,128)(2,1)S(1)}, bf16[1024,768]{1,0:T(8,128)(2,1)S(1)}, bf16[1024,768]{1,0:T(8,128)(2,1)S(1)}, f32[2,768]{1,0:T(2,128)S(1)}) custom-call(s32[4]{0:T(128)S(1)} %copy-done.31, s32[1]{0:T(128)S(6)} %copy.35.pln, bf16[1024,2304]{1,0:T(8,128)(2,1)S(1)} %bitcast.97, bf16[1024,2304]{1,0:T(8,128)(2,1)S(1)} %bitcast.97, ...), custom_call_target="tpu_custom_call" | custom-call | flops 10066329600 | bytes 12582912 | tf_op jit(solution)/shard_map/pallas_call | solution.py:340
  239.9 4.0 copy-done.1
  247.1 4.4 %shard_map.227 = f32[768,2304]{1,0:T(8,128)S(1)} custom-call(bf16[512,768]{1,0:T(8,128)(2,1)S(1)} %bitcast.90, bf16[512,768]{1,0:T(8,128)(2,1)S(1)} %bitcast.93, bf16[1024,768]{1,0:T(8,128)(2,1)S(1)} %get-tuple-element.85.a.refs_2_, bf16[1024,768]{1,0:T(8,128)(2,1)S(1)} %copy-done.35, bf16[1024,768]{1,0:T(8,128)(2,1)S(1)} %copy-done.38), custom_call_target="tpu_custom_call" | custom-call | flops 3623878656 | bytes 13369344 | tf_op jit(solution)/shard_map/pallas_call | solution.py:563
  254.4 8.3 %shard_map.239 = f32[3072,768]{1,0:T(8,128)S(1)} custom-call(bf16[1024,3072]{1,0:T(8,128)(2,1)S(1)} %bitcast.95, bf16[1024,768]{1,0:T(8,128)(2,1)S(1)} %copy-done.53), custom_call_target="tpu_custom_call" | custom-call | flops 4831838208 | bytes 17301504 | tf_op jit(solution)/shard_map/pallas_call | solution.py:563
  264.4 3.3 copy-done.2
  285.5 20.2 %collective-permute-done.24.b2 = bf16[4,24,768]{2,1,0:T(8,128)(2,1)S(1)} collective-permute-done((bf16[4,24,768]{2,1,0:T(8,128)(2,1)S(1)}, bf16[4,24,768]{2,1,0:T(8,128)(2,1)S(1)}, u32[]{:S(2)}, u32[]{:S(2)}) %collective-permute-start.24) | collective-permute-done | bytes 147488 | tf_op jit(solution)/shard_map/ppermute | solution.py:70
  306.7 3.3 collective-permute-start.26
  317.6 5.6 %shard_map.226 = (bf16[512,768]{1,0:T(8,128)(2,1)}, bf16[512,768]{1,0:T(8,128)(2,1)}) custom-call(f32[1024,768]{1,0:T(8,128)S(1)} %copy-done.55, bf16[1024,768]{1,0:T(8,128)(2,1)S(1)} %copy-done.33, bf16[1024,768]{1,0:T(8,128)(2,1)S(1)} %copy-done.36, bf16[1024,768]{1,0:T(8,128)(2,1)S(1)} %copy-done.39, bf16[768,2304]{1,0:T(8,128)(2,1)S(1)} %bitcast.83), custom_call_target="tpu_custom_call" | custom-call | flops 3623878656 | bytes 9437184 | tf_op jit(solution)/shard_map/pallas_call | solution.py:592
  325.1 3.8 collective-permute-start.19
  341.8 4.9 %collective-permute-done.30.b1 = bf16[4,24,3072]{2,1,0:T(8,128)(2,1)S(1)} collective-permute-done((bf16[4,24,3072]{2,1,0:T(8,128)(2,1)S(1)}, bf16[4,24,3072]{2,1,0:T(8,128)(2,1)S(1)}, u32[]{:S(2)}, u32[]{:S(2)}) %collective-permute-start.30) | collective-permute-done | bytes 589856 | tf_op jit(solution)/shard_map/ppermute | solution.py:70
  346.7 13.6 %collective-permute-done.31.b2 = bf16[4,24,3072]{2,1,0:T(8,128)(2,1)S(1)} collective-permute-done((bf16[4,24,3072]{2,1,0:T(8,128)(2,1)S(1)}, bf16[4,24,3072]{2,1,0:T(8,128)(2,1)S(1)}, u32[]{:S(2)}, u32[]{:S(2)}) %collective-permute-start.31) | collective-permute-done | bytes 589856 | tf_op jit(solution)/shard_map/ppermute | solution.py:70
  361.4 3.8 collective-permute-start.33
  365.7 6.4 %collective-permute-done.37.b1 = bf16[4,96,768]{2,1,0:T(8,128)(2,1)S(1)} collective-permute-done((bf16[4,96,768]{2,1,0:T(8,128)(2,1)S(1)}, bf16[4,96,768]{2,1,0:T(8,128)(2,1)S(1)}, u32[]{:S(2)}, u32[]{:S(2)}) %collective-permute-start.37) | collective-permute-done | bytes 589856 | tf_op jit(solution)/shard_map/ppermute | solution.py:70
  372.1 8.9 %collective-permute-done.38.b2 = bf16[4,96,768]{2,1,0:T(8,128)(2,1)S(1)} collective-permute-done((bf16[4,96,768]{2,1,0:T(8,128)(2,1)S(1)}, bf16[4,96,768]{2,1,0:T(8,128)(2,1)S(1)}, u32[]{:S(2)}, u32[]{:S(2)}) %collective-permute-start.38) | collective-permute-done | bytes 589856 | tf_op jit(solution)/shard_map/ppermute | solution.py:70
  382.0 3.5 collective-permute-start.40
  386.3 4.4 %collective-permute-done.41 = bf16[1,96,768]{2,1,0:T(8,128)(2,1)S(1)} collective-permute-done((bf16[1,96,768]{2,1,0:T(8,128)(2,1)S(1)}, bf16[1,96,768]{2,1,0:T(8,128)(2,1)S(1)}, u32[]{:S(2)}, u32[]{:S(2)}) %collective-permute-start.41) | collective-permute-done | bytes 147488 | tf_op jit(solution)/shard_map/ppermute | solution.py:70
  (262 shorter events, 115.9 us)
Async XLA Ops:
  7.2 134.7 %all-gather.2.cloned.1.call-start = ((), (), s32[]{:S(2)}) async-start(), calls=%async_computation | async-start | bytes 4866048 | tf_op jit(solution)/shard_map/all_gather | solution.py:616
  13.8 13.3 %collective-permute-start.2 = (bf16[1,24,2432]{2,1,0:T(8,128)(2,1)S(1)}, bf16[1,24,2432]{2,1,0:T(8,128)(2,1)S(1)}, u32[]{:S(2)}, u32[]{:S(2)}) collective-permute-start(bf16[1,24,2432]{2,1,0:T(8,128)(2,1)S(1)} %maximum_bitcast_fusion.refs_0_), channel_id=1, source_target_pairs={{0,24},{1,25},{2,26},{3,27},{4,28},{5,29},{6,30},{7,31},{8,16},{9,... | collective-permute-start | bytes 350216 | tf_op jit(solution)/shard_map/ppermute | solution.py:70
  27.1 28.9 %collective-permute-start.3 = (bf16[4,24,2432]{2,1,0:T(8,128)(2,1)S(1)}, bf16[4,24,2432]{2,1,0:T(8,128)(2,1)S(1)}, u32[]{:S(2)}, u32[]{:S(2)}) collective-permute-start(bf16[4,24,2432]{2,1,0:T(8,128)(2,1)S(1)} %shard_map.212.refs_0_), channel_id=1, source_target_pairs={{0,2},{1,3},{2,0},{3,1},{4,6},{5,7},{6,4},{7,5},{8,10},{9,11},{10,... | collective-permute-start | bytes 1400840 | tf_op jit(solution)/shard_map/ppermute | solution.py:70
  29.5 17.4 %collective-permute-start.8 = (bf16[1,24,3840]{2,1,0:T(8,128)(2,1)S(1)}, bf16[1,24,3840]{2,1,0:T(8,128)(2,1)S(1)}, u32[]{:S(2)}, u32[]{:S(2)}) collective-permute-start(bf16[1,24,3840]{2,1,0:T(8,128)(2,1)S(1)} %bitcast.77), channel_id=1, source_target_pairs={{0,16},{1,17},{2,18},{3,19},{4,20},{5,21},{6,22},{7,23},{8,24},{9,... | collective-permute-start | bytes 552968 | tf_op jit(solution)/shard_map/ppermute | solution.py:70
  31.0 22.5 %collective-permute-start.9 = (bf16[1,24,3840]{2,1,0:T(8,128)(2,1)S(1)}, bf16[1,24,3840]{2,1,0:T(8,128)(2,1)S(1)}, u32[]{:S(2)}, u32[]{:S(2)}) collective-permute-start(bf16[1,24,3840]{2,1,0:T(8,128)(2,1)S(1)} %bitcast.78), channel_id=1, source_target_pairs={{0,24},{1,25},{2,26},{3,27},{4,28},{5,29},{6,30},{7,31},{8,16},{9,... | collective-permute-start | bytes 552968 | tf_op jit(solution)/shard_map/ppermute | solution.py:70
  33.0 24.1 %collective-permute-start.4 = (bf16[4,24,2432]{2,1,0:T(8,128)(2,1)S(1)}, bf16[4,24,2432]{2,1,0:T(8,128)(2,1)S(1)}, u32[]{:S(2)}, u32[]{:S(2)}) collective-permute-start(bf16[4,24,2432]{2,1,0:T(8,128)(2,1)S(1)} %shard_map.212.refs_0_), channel_id=1, source_target_pairs={{0,4},{1,5},{2,6},{3,7},{4,0},{5,1},{6,2},{7,3},{8,12},{9,13},{10,... | collective-permute-start | bytes 1400840 | tf_op jit(solution)/shard_map/ppermute | solution.py:70
  37.1 23.7 %collective-permute-start.5 = (bf16[4,24,2432]{2,1,0:T(8,128)(2,1)S(1)}, bf16[4,24,2432]{2,1,0:T(8,128)(2,1)S(1)}, u32[]{:S(2)}, u32[]{:S(2)}) collective-permute-start(bf16[4,24,2432]{2,1,0:T(8,128)(2,1)S(1)} %shard_map.212.refs_0_), channel_id=1, source_target_pairs={{0,6},{1,7},{2,4},{3,5},{4,2},{5,3},{6,0},{7,1},{8,14},{9,15},{10,... | collective-permute-start | bytes 1400840 | tf_op jit(solution)/shard_map/ppermute | solution.py:70
  53.5 31.4 %collective-permute-start.10 = (bf16[4,24,3840]{2,1,0:T(8,128)(2,1)S(1)}, bf16[4,24,3840]{2,1,0:T(8,128)(2,1)S(1)}, u32[]{:S(2)}, u32[]{:S(2)}) collective-permute-start(bf16[4,24,3840]{2,1,0:T(8,128)(2,1)S(1)} %shard_map.217.refs_0_), channel_id=1, source_target_pairs={{0,2},{1,3},{2,0},{3,1},{4,6},{5,7},{6,4},{7,5},{8,10},{9,11},{10,... | collective-permute-start | bytes 2211848 | tf_op jit(solution)/shard_map/ppermute | solution.py:70
  53.9 31.2 %collective-permute-start.11 = (bf16[4,24,3840]{2,1,0:T(8,128)(2,1)S(1)}, bf16[4,24,3840]{2,1,0:T(8,128)(2,1)S(1)}, u32[]{:S(2)}, u32[]{:S(2)}) collective-permute-start(bf16[4,24,3840]{2,1,0:T(8,128)(2,1)S(1)} %shard_map.217.refs_0_), channel_id=1, source_target_pairs={{0,4},{1,5},{2,6},{3,7},{4,0},{5,1},{6,2},{7,3},{8,12},{9,13},{10,... | collective-permute-start | bytes 2211848 | tf_op jit(solution)/shard_map/ppermute | solution.py:70
  56.0 41.0 %collective-permute-start.12 = (bf16[4,24,3840]{2,1,0:T(8,128)(2,1)S(1)}, bf16[4,24,3840]{2,1,0:T(8,128)(2,1)S(1)}, u32[]{:S(2)}, u32[]{:S(2)}) collective-permute-start(bf16[4,24,3840]{2,1,0:T(8,128)(2,1)S(1)} %shard_map.217.refs_0_), channel_id=1, source_target_pairs={{0,6},{1,7},{2,4},{3,5},{4,2},{5,3},{6,0},{7,1},{8,14},{9,15},{10,... | collective-permute-start | bytes 2211848 | tf_op jit(solution)/shard_map/ppermute | solution.py:70
  60.9 37.1 %collective-permute-start.6 = (bf16[16,24,2432]{2,1,0:T(8,128)(2,1)S(1)}, bf16[16,24,2432]{2,1,0:T(8,128)(2,1)S(1)}, u32[]{:S(2)}, u32[]{:S(2)}) collective-permute-start(bf16[16,24,2432]{2,1,0:T(8,128)(2,1)S(1)} %shard_map.213.refs_0_), channel_id=1, source_target_pairs={{0,1},{1,0},{2,3},{3,2},{4,5},{5,4},{6,7},{7,6},{8,9},{9,8},{10,11... | collective-permute-start | bytes 5603336 | tf_op jit(solution)/shard_map/ppermute | solution.py:70
  97.2 32.1 %collective-permute-start.13 = (bf16[16,24,3840]{2,1,0:T(8,128)(2,1)S(1)}, bf16[16,24,3840]{2,1,0:T(8,128)(2,1)}, u32[]{:S(2)}, u32[]{:S(2)}) collective-permute-start(bf16[16,24,3840]{2,1,0:T(8,128)(2,1)S(1)} %shard_map.218.refs_0_), channel_id=1, source_target_pairs={{0,1},{1,0},{2,3},{3,2},{4,5},{5,4},{6,7},{7,6},{8,9},{9,8},{10,11... | collective-permute-start | bytes 8847368 | tf_op jit(solution)/shard_map/ppermute | solution.py:70
  245.6 37.5 %collective-permute-start.28 = (bf16[16,24,3072]{2,1,0:T(8,128)(2,1)}, bf16[16,24,3072]{2,1,0:T(8,128)(2,1)S(1)}, u32[]{:S(2)}, u32[]{:S(2)}) collective-permute-start(bf16[16,24,3072]{2,1,0:T(8,128)(2,1)} %shard_map.236), channel_id=1, source_target_pairs={{0,1},{1,0},{2,3},{3,2},{4,5},{5,4},{6,7},{7,6},{8,9},{9,8},{10,11... | collective-permute-start | bytes 7077896 | tf_op jit(solution)/shard_map/ppermute | solution.py:70
  253.6 22.8 %collective-permute-start.14 = (bf16[16,24,2432]{2,1,0:T(8,128)(2,1)}, bf16[16,24,2432]{2,1,0:T(8,128)(2,1)S(1)}, u32[]{:S(2)}, u32[]{:S(2)}) collective-permute-start(bf16[16,24,2432]{2,1,0:T(8,128)(2,1)} %shard_map.228), channel_id=1, source_target_pairs={{0,1},{1,0},{2,3},{3,2},{4,5},{5,4},{6,7},{7,6},{8,9},{9,8},{10,11... | collective-permute-start | bytes 5603336 | tf_op jit(solution)/shard_map/ppermute | solution.py:70
  267.7 62.7 %collective-permute-start.35 = (bf16[16,96,768]{2,1,0:T(8,128)(2,1)}, bf16[16,96,768]{2,1,0:T(8,128)(2,1)S(1)}, u32[]{:S(2)}, u32[]{:S(2)}) collective-permute-start(bf16[16,96,768]{2,1,0:T(8,128)(2,1)} %shard_map.240), channel_id=1, source_target_pairs={{0,1},{1,0},{2,3},{3,2},{4,5},{5,4},{6,7},{7,6},{8,9},{9,8},{10,11... | collective-permute-start | bytes 7077896 | tf_op jit(solution)/shard_map/ppermute | solution.py:70
  276.7 29.6 %collective-permute-start.15 = (bf16[4,24,2432]{2,1,0:T(8,128)(2,1)S(1)}, bf16[4,24,2432]{2,1,0:T(8,128)(2,1)S(1)}, u32[]{:S(2)}, u32[]{:S(2)}) collective-permute-start(bf16[4,24,2432]{2,1,0:T(8,128)(2,1)S(1)} %get-tuple-element.94), channel_id=1, source_target_pairs={{0,2},{1,3},{2,0},{3,1},{4,6},{5,7},{6,4},{7,5},{8,10},{9,11},{10,... | collective-permute-start | bytes 1400840 | tf_op jit(solution)/shard_map/ppermute | solution.py:70
  279.7 27.0 %collective-permute-start.16 = (bf16[4,24,2432]{2,1,0:T(8,128)(2,1)S(1)}, bf16[4,24,2432]{2,1,0:T(8,128)(2,1)S(1)}, u32[]{:S(2)}, u32[]{:S(2)}) collective-permute-start(bf16[4,24,2432]{2,1,0:T(8,128)(2,1)S(1)} %get-tuple-element.95), channel_id=1, source_target_pairs={{0,4},{1,5},{2,6},{3,7},{4,0},{5,1},{6,2},{7,3},{8,12},{9,13},{10,... | collective-permute-start | bytes 1400840 | tf_op jit(solution)/shard_map/ppermute | solution.py:70
  281.5 28.5 %collective-permute-start.17 = (bf16[4,24,2432]{2,1,0:T(8,128)(2,1)S(1)}, bf16[4,24,2432]{2,1,0:T(8,128)(2,1)S(1)}, u32[]{:S(2)}, u32[]{:S(2)}) collective-permute-start(bf16[4,24,2432]{2,1,0:T(8,128)(2,1)S(1)} %get-tuple-element.96), channel_id=1, source_target_pairs={{0,6},{1,7},{2,4},{3,5},{4,2},{5,3},{6,0},{7,1},{8,14},{9,15},{10,... | collective-permute-start | bytes 1400840 | tf_op jit(solution)/shard_map/ppermute | solution.py:70
  283.1 22.7 %collective-permute-start.24 = (bf16[4,24,768]{2,1,0:T(8,128)(2,1)S(1)}, bf16[4,24,768]{2,1,0:T(8,128)(2,1)S(1)}, u32[]{:S(2)}, u32[]{:S(2)}) collective-permute-start(bf16[4,24,768]{2,1,0:T(8,128)(2,1)S(1)} %get-tuple-element.104), channel_id=1, source_target_pairs={{0,6},{1,7},{2,4},{3,5},{4,2},{5,3},{6,0},{7,1},{8,14},{9,15},{10,... | collective-permute-start | bytes 442376 | tf_op jit(solution)/shard_map/ppermute | solution.py:70
  305.8 32.0 %collective-permute-start.29 = (bf16[4,24,3072]{2,1,0:T(8,128)(2,1)}, bf16[4,24,3072]{2,1,0:T(8,128)(2,1)S(1)}, u32[]{:S(2)}, u32[]{:S(2)}) collective-permute-start(bf16[4,24,3072]{2,1,0:T(8,128)(2,1)} %get-tuple-element.109), channel_id=1, source_target_pairs={{0,2},{1,3},{2,0},{3,1},{4,6},{5,7},{6,4},{7,5},{8,10},{9,11},{10,... | collective-permute-start | bytes 1769480 | tf_op jit(solution)/shard_map/ppermute | solution.py:70
  306.4 18.1 %collective-permute-start.27 = (bf16[1,24,768]{2,1,0:T(8,128)(2,1)S(1)}, bf16[1,24,768]{2,1,0:T(8,128)(2,1)}, u32[]{:S(2)}, u32[]{:S(2)}) collective-permute-start(bf16[1,24,768]{2,1,0:T(8,128)(2,1)S(1)} %get-tuple-element.108), channel_id=1, source_target_pairs={{0,24},{1,25},{2,26},{3,27},{4,28},{5,29},{6,30},{7,31},{8,16},{9,... | collective-permute-start | bytes 110600 | tf_op jit(solution)/shard_map/ppermute | solution.py:70
  306.7 18.4 %collective-permute-start.26 = (bf16[1,24,768]{2,1,0:T(8,128)(2,1)S(1)}, bf16[1,24,768]{2,1,0:T(8,128)(2,1)}, u32[]{:S(2)}, u32[]{:S(2)}) collective-permute-start(bf16[1,24,768]{2,1,0:T(8,128)(2,1)S(1)} %get-tuple-element.107), channel_id=1, source_target_pairs={{0,16},{1,17},{2,18},{3,19},{4,20},{5,21},{6,22},{7,23},{8,24},{9,... | collective-permute-start | bytes 110600 | tf_op jit(solution)/shard_map/ppermute | solution.py:70
  310.9 18.1 %collective-permute-start.25 = (bf16[1,24,768]{2,1,0:T(8,128)(2,1)S(1)}, bf16[1,24,768]{2,1,0:T(8,128)(2,1)}, u32[]{:S(2)}, u32[]{:S(2)}) collective-permute-start(bf16[1,24,768]{2,1,0:T(8,128)(2,1)S(1)} %get-tuple-element.106), channel_id=1, source_target_pairs={{0,8},{1,9},{2,10},{3,11},{4,12},{5,13},{6,14},{7,15},{8,0},{9,1},... | collective-permute-start | bytes 110600 | tf_op jit(solution)/shard_map/ppermute | solution.py:70
  325.1 11.3 %collective-permute-start.19 = (bf16[1,24,2432]{2,1,0:T(8,128)(2,1)S(1)}, bf16[1,24,2432]{2,1,0:T(8,128)(2,1)S(1)}, u32[]{:S(2)}, u32[]{:S(2)}) collective-permute-start(bf16[1,24,2432]{2,1,0:T(8,128)(2,1)S(1)} %get-tuple-element.99), channel_id=1, source_target_pairs={{0,16},{1,17},{2,18},{3,19},{4,20},{5,21},{6,22},{7,23},{8,24},{9,... | collective-permute-start | bytes 350216 | tf_op jit(solution)/shard_map/ppermute | solution.py:70
  330.4 16.3 %collective-permute-start.30 = (bf16[4,24,3072]{2,1,0:T(8,128)(2,1)S(1)}, bf16[4,24,3072]{2,1,0:T(8,128)(2,1)S(1)}, u32[]{:S(2)}, u32[]{:S(2)}) collective-permute-start(bf16[4,24,3072]{2,1,0:T(8,128)(2,1)S(1)} %copy-done.30), channel_id=1, source_target_pairs={{0,4},{1,5},{2,6},{3,7},{4,0},{5,1},{6,2},{7,3},{8,12},{9,13},{10,... | collective-permute-start | bytes 1769480 | tf_op jit(solution)/shard_map/ppermute | solution.py:70
  334.2 26.1 %collective-permute-start.31 = (bf16[4,24,3072]{2,1,0:T(8,128)(2,1)S(1)}, bf16[4,24,3072]{2,1,0:T(8,128)(2,1)S(1)}, u32[]{:S(2)}, u32[]{:S(2)}) collective-permute-start(bf16[4,24,3072]{2,1,0:T(8,128)(2,1)S(1)} %copy-done.28), channel_id=1, source_target_pairs={{0,6},{1,7},{2,4},{3,5},{4,2},{5,3},{6,0},{7,1},{8,14},{9,15},{10,... | collective-permute-start | bytes 1769480 | tf_op jit(solution)/shard_map/ppermute | solution.py:70
  336.4 28.8 %collective-permute-start.36 = (bf16[4,96,768]{2,1,0:T(8,128)(2,1)S(1)}, bf16[4,96,768]{2,1,0:T(8,128)(2,1)S(1)}, u32[]{:S(2)}, u32[]{:S(2)}) collective-permute-start(bf16[4,96,768]{2,1,0:T(8,128)(2,1)S(1)} %get-tuple-element.116), channel_id=1, source_target_pairs={{0,2},{1,3},{2,0},{3,1},{4,6},{5,7},{6,4},{7,5},{8,10},{9,11},{10,... | collective-permute-start | bytes 1769480 | tf_op jit(solution)/shard_map/ppermute | solution.py:70
  336.9 35.2 %collective-permute-start.37 = (bf16[4,96,768]{2,1,0:T(8,128)(2,1)S(1)}, bf16[4,96,768]{2,1,0:T(8,128)(2,1)S(1)}, u32[]{:S(2)}, u32[]{:S(2)}) collective-permute-start(bf16[4,96,768]{2,1,0:T(8,128)(2,1)S(1)} %get-tuple-element.117), channel_id=1, source_target_pairs={{0,4},{1,5},{2,6},{3,7},{4,0},{5,1},{6,2},{7,3},{8,12},{9,13},{10,... | collective-permute-start | bytes 1769480 | tf_op jit(solution)/shard_map/ppermute | solution.py:70
  337.7 43.3 %collective-permute-start.38 = (bf16[4,96,768]{2,1,0:T(8,128)(2,1)S(1)}, bf16[4,96,768]{2,1,0:T(8,128)(2,1)S(1)}, u32[]{:S(2)}, u32[]{:S(2)}) collective-permute-start(bf16[4,96,768]{2,1,0:T(8,128)(2,1)S(1)} %get-tuple-element.118), channel_id=1, source_target_pairs={{0,6},{1,7},{2,4},{3,5},{4,2},{5,3},{6,0},{7,1},{8,14},{9,15},{10,... | collective-permute-start | bytes 1769480 | tf_op jit(solution)/shard_map/ppermute | solution.py:70
  360.7 24.8 %collective-permute-start.34 = (bf16[1,24,3072]{2,1,0:T(8,128)(2,1)S(1)}, bf16[1,24,3072]{2,1,0:T(8,128)(2,1)S(1)}, u32[]{:S(2)}, u32[]{:S(2)}) collective-permute-start(bf16[1,24,3072]{2,1,0:T(8,128)(2,1)S(1)} %get-tuple-element.115), channel_id=1, source_target_pairs={{0,24},{1,25},{2,26},{3,27},{4,28},{5,29},{6,30},{7,31},{8,16},{9,... | collective-permute-start | bytes 442376 | tf_op jit(solution)/shard_map/ppermute | solution.py:70
  361.4 24.1 %collective-permute-start.33 = (bf16[1,24,3072]{2,1,0:T(8,128)(2,1)S(1)}, bf16[1,24,3072]{2,1,0:T(8,128)(2,1)S(1)}, u32[]{:S(2)}, u32[]{:S(2)}) collective-permute-start(bf16[1,24,3072]{2,1,0:T(8,128)(2,1)S(1)} %get-tuple-element.114), channel_id=1, source_target_pairs={{0,16},{1,17},{2,18},{3,19},{4,20},{5,21},{6,22},{7,23},{8,24},{9,... | collective-permute-start | bytes 442376 | tf_op jit(solution)/shard_map/ppermute | solution.py:70
  365.2 20.4 %collective-permute-start.32 = (bf16[1,24,3072]{2,1,0:T(8,128)(2,1)S(1)}, bf16[1,24,3072]{2,1,0:T(8,128)(2,1)S(1)}, u32[]{:S(2)}, u32[]{:S(2)}) collective-permute-start(bf16[1,24,3072]{2,1,0:T(8,128)(2,1)S(1)} %get-tuple-element.113), channel_id=1, source_target_pairs={{0,8},{1,9},{2,10},{3,11},{4,12},{5,13},{6,14},{7,15},{8,0},{9,1},... | collective-permute-start | bytes 442376 | tf_op jit(solution)/shard_map/ppermute | solution.py:70
  (79 other events, 585.2 us)
Sparse Core Ops, SparseCore 0:
  10.9 76.8 all-gather.1
